TPU v7x, 32 devices: a whole 2x2x4 slice. The times are simulated.
32 devices in a mesh: lat: 8 (over z, core), lon: 4 (over y, x).
Axes of the slice: x: 2, y: 2, z: 4, core: 2. Of those that a mesh axis runs over, the one named last changes fastest.
Arguments:
- ensemble: float32 [80, 1, 256, 512], P(None, None, 'lat', 'lon'), may hold values from -6 to 6
- obs_value: float32 [4, 8, 4, 128], P(None, 'lat', 'lon'), may hold values from -6 to 6
- obs_error: float32 [4, 8, 4, 128], P(None, 'lat', 'lon'), may hold values from 0.25 to 4
- obs_cell: int32 [4, 8, 4, 128], P(None, 'lat', 'lon'), may hold values from 0 to 4095
- obs_radius: int32 [4, 8, 4, 128], P(None, 'lat', 'lon'), may hold values from 8 to 32
- obs_count: int32 [4, 8, 4], P(None, 'lat', 'lon'), may hold values from 16 to 128, as said below
- batch_order: int32 [4], replicated, may hold values from 0 to 3, each once
Outputs:
- analysis: float32 [80, 1, 256, 512], P(None, None, 'lat', 'lon')
Inputs may be any that keep to these rules, and one draw needn't show every extreme that they name: `obs_count`: slots at or beyond the count hold no observation and are ignored. In every batch some tile has all 128 slots live.
All inputs are finite; a program needn't handle non-finite values.
Results may differ from a plain program's by a relative error of at most 0.0021.
Values may be sent and summed in bfloat16 or wider, within the bound.
A program may use at most 64 MiB of HBM per device.

v0:
```python
import math

import jax
import jax.numpy as jnp
from jax import lax
from jax.sharding import PartitionSpec as P


def shifted(value, axis, steps):
    count = lax.axis_size(axis)
    leading, last = (max(0, -steps), min(count, count - steps))
    return lax.ppermute(value, axis, [(source, source + steps) for source in range(leading, last)])


def passed_along(value, axis, steps):
    count = lax.axis_size(axis)
    pairs = [(source, (source + steps) % count) for source in range(count)]
    return lax.ppermute(value, axis, pairs)


def observe_stats(priors, values, errors, is_live):
    members = priors.shape[0]
    prior_mean = jnp.mean(priors, axis=0)
    spread = priors - prior_mean
    variance = jnp.sum(spread * spread, axis=0) / (members - 1)
    denom_total = variance + errors
    shrink = 1.0 / (1.0 + jnp.sqrt(errors / denom_total))
    factor = 1.0 / ((members - 1) * denom_total)
    obs_pert = jnp.where(is_live, spread, 0.0).astype(jnp.bfloat16)
    obs_gain = jnp.where(is_live, factor * (values - prior_mean - shrink * spread), 0.0).astype(
        jnp.bfloat16
    )
    return (obs_pert, obs_gain)


def assimilate(current, obs_pert, obs_gain, where_ints, lat_base, lon_base, full_lon, block_cols):
    members, levels, lat_rows, lon_cols = current.shape
    cells = lat_rows * lon_cols
    flat_state = current.reshape(members, levels, cells)
    centered = (flat_state - jnp.mean(flat_state, axis=0)).astype(jnp.bfloat16)
    obs_lat = where_ints[0]
    obs_lon = where_ints[1]
    cutoff = where_ints[2]
    cutoff_sq = cutoff * cutoff
    width_sq = jnp.maximum(cutoff_sq, 1).astype(jnp.float32)

    def one_block(block_id, total_inc):
        first_col = block_id * block_cols
        positions = first_col + jnp.arange(block_cols, dtype=jnp.int32)
        cell_lat = lat_base + positions // lon_cols
        cell_lon = lon_base + positions % lon_cols
        lat_gap = cell_lat[:, None] - obs_lat[None, :]
        lon_gap = jnp.abs(cell_lon[:, None] - obs_lon[None, :])
        lon_dist = jnp.minimum(lon_gap, full_lon - lon_gap)
        dist_sq = lat_gap * lat_gap + lon_dist * lon_dist
        weights = jnp.where(
            dist_sq <= cutoff_sq[None, :],
            jnp.exp(-2.0 * dist_sq.astype(jnp.float32) / width_sq[None, :]),
            0.0,
        )
        centered_block = lax.dynamic_slice_in_dim(centered, first_col, block_cols, 2).reshape(
            members, levels * block_cols
        )
        covariance = lax.dot_general(
            centered_block, obs_pert, (((0,), (0,)), ((), ())), preferred_element_type=jnp.float32
        )
        scaled = (
            (covariance.reshape(levels, block_cols, -1) * weights[None])
            .astype(jnp.bfloat16)
            .reshape(levels * block_cols, -1)
        )
        increment = lax.dot_general(
            obs_gain, scaled, (((1,), (1,)), ((), ())), preferred_element_type=jnp.float32
        )
        return lax.dynamic_update_slice_in_dim(
            total_inc, increment.reshape(members, levels, block_cols), first_col, 2
        )

    total_inc = lax.fori_loop(0, cells // block_cols, one_block, jnp.zeros_like(flat_state))
    return (flat_state + total_inc).reshape(current.shape)


def from_lat(packed, offset):
    return shifted((packed[0], packed[1]), "lat", offset)


def from_lon(packed, offset):
    return passed_along((packed[0], packed[1]), "lon", offset)


def local(ensemble, obs_value, obs_error, obs_cell, obs_radius, obs_count, batch_order):
    members, levels, lat_rows, lon_cols = ensemble.shape
    lon_devices = lax.axis_size("lon")
    lon_here = lax.axis_index("lon")
    lat_base = lax.axis_index("lat") * lat_rows
    lon_base = lon_here * lon_cols
    full_lon = lon_cols * lon_devices
    block_cols = math.gcd(1024, lat_rows * lon_cols)
    slot_total = obs_cell.shape[-1]
    slot_ids = jnp.arange(slot_total, dtype=jnp.int32)
    current = ensemble
    for batch_step in range(obs_cell.shape[0]):
        chosen = batch_order[batch_step]
        cell_ids = obs_cell[chosen, 0, 0]
        surface = current[:, 0].reshape(members, lat_rows * lon_cols)
        priors = jnp.take(surface, cell_ids, axis=1)
        is_live = slot_ids < obs_count[chosen, 0, 0]
        obs_pert, obs_gain = observe_stats(
            priors, obs_value[chosen, 0, 0], obs_error[chosen, 0, 0], is_live
        )
        floats_here = jnp.stack([obs_pert, obs_gain])
        ints_here = jnp.stack(
            [
                lat_base + cell_ids // lon_cols,
                lon_base + cell_ids % lon_cols,
                obs_radius[chosen, 0, 0],
            ]
        )
        lower_band = from_lat((floats_here, ints_here), 1)
        upper_band = from_lat((floats_here, ints_here), -1)
        floats_band = jnp.stack([lower_band[0], floats_here, upper_band[0]])
        ints_band = jnp.stack([lower_band[1], ints_here, upper_band[1]])
        western = from_lon((floats_band, ints_band), 1)
        eastern = from_lon((floats_band, ints_band), -1)
        floats_near = jnp.stack([western[0], floats_band, eastern[0]])
        ints_near = jnp.stack([western[1], ints_band, eastern[1]])
        count_obs = 9 * slot_total
        pert_near = jnp.transpose(floats_near[:, :, 0], (2, 0, 1, 3)).reshape(members, count_obs)
        gain_near = jnp.transpose(floats_near[:, :, 1], (2, 0, 1, 3)).reshape(members, count_obs)
        where_near = jnp.transpose(ints_near, (2, 0, 1, 3)).reshape(3, count_obs)
        current = assimilate(
            current, pert_near, gain_near, where_near, lat_base, lon_base, full_lon, block_cols
        )
    return current


def solution(mesh):
    return jax.shard_map(
        local,
        mesh=mesh,
        in_specs=(
            P(None, None, "lat", "lon"),
            P(None, "lat", "lon", None),
            P(None, "lat", "lon", None),
            P(None, "lat", "lon", None),
            P(None, "lat", "lon", None),
            P(None, "lat", "lon"),
            P(),
        ),
        out_specs=P(None, None, "lat", "lon"),
        check_vma=False,
    )
```

profile of v0, /device:TPU:17, one launch (start us, length us, event | category | flops | bytes accessed | tf_op | source)
XLA Modules:
  0.0 237.1 jit_solution(3778791868117569262)
XLA Ops:
  17.1 3.8 %collective-permute-start = (bf16[2,80,128]{1,2,0:T(8,128)(2,1)}, bf16[2,80,128]{1,2,0:T(8,128)(2,1)}, u32[]{:S(2)}, u32[]{:S(2)}) collective-permute-start(bf16[2,80,128]{1,2,0:T(8,128)(2,1)} %get-tuple-element.1307), channel_id=1, source_target_pairs={{0,4},{4,8},{8,12},{12,16},{16,20},{20,24},{24,28},{1,5},{5,9},{9,... | collective-permute-start | bytes 122888 | tf_op jit(solution)/shard_map/ppermute | solution.py:12
  22.9 3.6 %collective-permute-start.4 = (s32[3,128]{1,0:T(4,128)S(1)}, s32[3,128]{1,0:T(4,128)S(1)}, u32[]{:S(2)}, u32[]{:S(2)}) collective-permute-start(s32[3,128]{1,0:T(4,128)S(1)} %get-tuple-element.1361), channel_id=1, source_target_pairs={{0,4},{4,8},{8,12},{12,16},{16,20},{20,24},{24,28},{1,5},{5,9},{9,... | collective-permute-start | bytes 4616 | tf_op jit(solution)/shard_map/ppermute | solution.py:12
  28.5 3.6 %collective-permute-start.12 = (s32[3,128]{1,0:T(4,128)S(1)}, s32[3,128]{1,0:T(4,128)S(1)}, u32[]{:S(2)}, u32[]{:S(2)}) collective-permute-start(s32[3,128]{1,0:T(4,128)S(1)} %get-tuple-element.1359), channel_id=1, source_target_pairs={{0,4},{4,8},{8,12},{12,16},{16,20},{20,24},{24,28},{1,5},{5,9},{9,... | collective-permute-start | bytes 4616 | tf_op jit(solution)/shard_map/ppermute | solution.py:12
  39.2 2.5 %collective-permute-start.21 = (s32[3,128]{1,0:T(4,128)S(1)}, s32[3,128]{1,0:T(4,128)S(1)}, u32[]{:S(2)}, u32[]{:S(2)}) collective-permute-start(s32[3,128]{1,0:T(4,128)S(1)} %get-tuple-element.1357), channel_id=1, source_target_pairs={{4,0},{8,4},{12,8},{16,12},{20,16},{24,20},{28,24},{5,1},{9,5},{13... | collective-permute-start | bytes 4616 | tf_op jit(solution)/shard_map/ppermute | solution.py:12
  41.7 3.1 %collective-permute-start.20 = (s32[3,128]{1,0:T(4,128)S(1)}, s32[3,128]{1,0:T(4,128)S(1)}, u32[]{:S(2)}, u32[]{:S(2)}) collective-permute-start(s32[3,128]{1,0:T(4,128)S(1)} %get-tuple-element.1357), channel_id=1, source_target_pairs={{0,4},{4,8},{8,12},{12,16},{16,20},{20,24},{24,28},{1,5},{5,9},{9,... | collective-permute-start | bytes 4616 | tf_op jit(solution)/shard_map/ppermute | solution.py:12
  44.9 2.4 %collective-permute-start.28 = (s32[3,128]{1,0:T(4,128)S(1)}, s32[3,128]{1,0:T(4,128)S(1)}, u32[]{:S(2)}, u32[]{:S(2)}) collective-permute-start(s32[3,128]{1,0:T(4,128)S(1)} %get-tuple-element.1355), channel_id=1, source_target_pairs={{0,4},{4,8},{8,12},{12,16},{16,20},{20,24},{24,28},{1,5},{5,9},{9,... | collective-permute-start | bytes 4616 | tf_op jit(solution)/shard_map/ppermute | solution.py:12
  63.9 2.4 collective-permute-start.2
  67.0 2.4 %collective-permute-done.2 = bf16[3,2,80,128]{2,3,1,0:T(8,128)(2,1)S(1)} collective-permute-done((bf16[3,2,80,128]{2,3,1,0:T(8,128)(2,1)S(1)}, bf16[3,2,80,128]{2,3,1,0:T(8,128)(2,1)S(1)}, u32[]{:S(2)}, u32[]{:S(2)}) %collective-permute-start.2) | collective-permute-done | bytes 122912 | tf_op jit(solution)/shard_map/ppermute | solution.py:18
  69.4 3.2 %collective-permute-done.3 = bf16[3,2,80,128]{2,3,1,0:T(8,128)(2,1)S(1)} collective-permute-done((bf16[3,2,80,128]{2,3,1,0:T(8,128)(2,1)S(1)}, bf16[3,2,80,128]{2,3,1,0:T(8,128)(2,1)S(1)}, u32[]{:S(2)}, u32[]{:S(2)}) %collective-permute-start.3) | collective-permute-done | bytes 122912 | tf_op jit(solution)/shard_map/ppermute | solution.py:18
  73.3 14.6 %while.60 = (s32[]{:T(128)}, f32[80,1,4096]{2,0,1:T(8,128)S(1)}, bf16[80,1,4096]{2,0,1:T(8,128)(2,1)S(1)}, bf16[80,1152]{1,0:T(8,128)(2,1)S(1)}, s32[]{:T(128)},...) while((s32[]{:T(128)}, f32[80,1,4096]{2,0,1:T(8,128)S(1)}, ...), condition=%wide.region_4.6_spmd, body=%wide.region_3.5_spmd.sunk | while | flops 395204608 | bytes 928975 | solution.py:79
  73.4 3.6 %fusion.185 = f32[80,1,4096]{2,0,1:T(8,128)S(1)} fusion(f32[80,1,4096]{2,0,1:T(8,128)S(1)} %get-tuple-element.1688, s32[]{:T(128)S(6)} %select_n.593, bf16[80,1152]{1,0:T(8,128)(2,1)S(1)} %get-tuple-element.1712, bf16[80,1152]{1,0:T(8,128)(2,1)S(1)} %get-tuple-element.1705, f32[1152]{0:T(1024)S(1)} %get-tuple-element.1711, ...), kind=kOutput, calls=%fused_computation.12.clone.1 | convolution fusion | flops 395182080 | bytes 902144 | tf_op jit(solution)/shard_map/while/body/eval_jaxpr/dot_general | solution.py:72
  77.0 3.6 %fusion.185 = f32[80,1,4096]{2,0,1:T(8,128)S(1)} fusion(f32[80,1,4096]{2,0,1:T(8,128)S(1)} %get-tuple-element.1688, s32[]{:T(128)S(6)} %select_n.593, bf16[80,1152]{1,0:T(8,128)(2,1)S(1)} %get-tuple-element.1712, bf16[80,1152]{1,0:T(8,128)(2,1)S(1)} %get-tuple-element.1705, f32[1152]{0:T(1024)S(1)} %get-tuple-element.1711, ...), kind=kOutput, calls=%fused_computation.12.clone.1 | convolution fusion | flops 395182080 | bytes 902144 | tf_op jit(solution)/shard_map/while/body/eval_jaxpr/dot_general | solution.py:72
  80.7 3.6 %fusion.185 = f32[80,1,4096]{2,0,1:T(8,128)S(1)} fusion(f32[80,1,4096]{2,0,1:T(8,128)S(1)} %get-tuple-element.1688, s32[]{:T(128)S(6)} %select_n.593, bf16[80,1152]{1,0:T(8,128)(2,1)S(1)} %get-tuple-element.1712, bf16[80,1152]{1,0:T(8,128)(2,1)S(1)} %get-tuple-element.1705, f32[1152]{0:T(1024)S(1)} %get-tuple-element.1711, ...), kind=kOutput, calls=%fused_computation.12.clone.1 | convolution fusion | flops 395182080 | bytes 902144 | tf_op jit(solution)/shard_map/while/body/eval_jaxpr/dot_general | solution.py:72
  84.3 3.6 %fusion.185 = f32[80,1,4096]{2,0,1:T(8,128)S(1)} fusion(f32[80,1,4096]{2,0,1:T(8,128)S(1)} %get-tuple-element.1688, s32[]{:T(128)S(6)} %select_n.593, bf16[80,1152]{1,0:T(8,128)(2,1)S(1)} %get-tuple-element.1712, bf16[80,1152]{1,0:T(8,128)(2,1)S(1)} %get-tuple-element.1705, f32[1152]{0:T(1024)S(1)} %get-tuple-element.1711, ...), kind=kOutput, calls=%fused_computation.12.clone.1 | convolution fusion | flops 395182080 | bytes 902144 | tf_op jit(solution)/shard_map/while/body/eval_jaxpr/dot_general | solution.py:72
  89.7 2.8 %fusion.147 = (f32[4096]{0:T(1024)S(1)}, f32[80,1,4096]{0,2,1:T(8,128)S(1)}) fusion(f32[80,1,4096]{0,2,1:T(8,128)} %copy.32, f32[80,1,32,128]{0,3,2,1:T(8,128)} %copy-done), kind=kLoop, calls=%fused_computation.312 | loop fusion | flops 651264 | bytes 3948544 | tf_op jit(solution)/shard_map/reduce_sum | solution.py:40
  95.2 6.0 %collective-permute-start.8 = (bf16[2,80,128]{1,2,0:T(8,128)(2,1)S(1)}, bf16[2,80,128]{1,2,0:T(8,128)(2,1)S(1)}, u32[]{:S(2)}, u32[]{:S(2)}) collective-permute-start(bf16[2,80,128]{1,2,0:T(8,128)(2,1)S(1)} %get-tuple-element.1305), channel_id=1, source_target_pairs={{0,4},{4,8},{8,12},{12,16},{16,20},{20,24},{24,28},{1,5},{5,9},{9,... | collective-permute-start | bytes 122888 | tf_op jit(solution)/shard_map/ppermute | solution.py:12
  103.2 3.6 %collective-permute-done.9 = bf16[2,80,128]{1,2,0:T(8,128)(2,1)S(1)} collective-permute-done((bf16[2,80,128]{1,2,0:T(8,128)(2,1)S(1)}, bf16[2,80,128]{1,2,0:T(8,128)(2,1)S(1)}, u32[]{:S(2)}, u32[]{:S(2)}) %collective-permute-start.9) | collective-permute-done | bytes 40992 | tf_op jit(solution)/shard_map/ppermute | solution.py:12
  112.1 3.5 %collective-permute-done.10 = bf16[3,2,80,128]{2,3,1,0:T(8,128)(2,1)S(1)} collective-permute-done((bf16[3,2,80,128]{2,3,1,0:T(8,128)(2,1)}, bf16[3,2,80,128]{2,3,1,0:T(8,128)(2,1)S(1)}, u32[]{:S(2)}, u32[]{:S(2)}) %collective-permute-start.10) | collective-permute-done | bytes 122912 | tf_op jit(solution)/shard_map/ppermute | solution.py:18
  115.5 3.3 %collective-permute-done.11 = bf16[3,2,80,128]{2,3,1,0:T(8,128)(2,1)} collective-permute-done((bf16[3,2,80,128]{2,3,1,0:T(8,128)(2,1)}, bf16[3,2,80,128]{2,3,1,0:T(8,128)(2,1)}, u32[]{:S(2)}, u32[]{:S(2)}) %collective-permute-start.11) | collective-permute-done | bytes 122912 | tf_op jit(solution)/shard_map/ppermute | solution.py:18
  121.8 18.9 %while.61 = (s32[]{:T(128)}, f32[80,1,4096]{2,0,1:T(8,128)S(1)}, bf16[80,1,4096]{2,0,1:T(8,128)(2,1)}, bf16[80,1152]{1,0:T(8,128)(2,1)}, s32[]{:T(128)}, /*index...) while((s32[]{:T(128)}, f32[80,1,4096]{2,0,1:T(8,128)S(1)}, ...), condition=%wide.region_9.11_spmd, body=%wide.region_8.10_spmd.sunk | while | flops 395204608 | bytes 928975 | solution.py:79
  121.9 4.6 %fusion.190 = f32[80,1,4096]{2,0,1:T(8,128)S(1)} fusion(f32[80,1,4096]{2,0,1:T(8,128)S(1)} %get-tuple-element.1733, s32[]{:T(128)S(6)} %select_n.596, bf16[80,1152]{1,0:T(8,128)(2,1)} %get-tuple-element.1757, bf16[80,1152]{1,0:T(8,128)(2,1)} %get-tuple-element.1750, f32[1152]{0:T(1024)S(1)} %get-tuple-element.1756, ...), kind=kOutput, calls=%fused_computation.41.clone.1 | convolution fusion | flops 395182080 | bytes 902144 | tf_op jit(solution)/shard_map/while/body/eval_jaxpr/dot_general | solution.py:72
  126.7 4.6 %fusion.190 = f32[80,1,4096]{2,0,1:T(8,128)S(1)} fusion(f32[80,1,4096]{2,0,1:T(8,128)S(1)} %get-tuple-element.1733, s32[]{:T(128)S(6)} %select_n.596, bf16[80,1152]{1,0:T(8,128)(2,1)} %get-tuple-element.1757, bf16[80,1152]{1,0:T(8,128)(2,1)} %get-tuple-element.1750, f32[1152]{0:T(1024)S(1)} %get-tuple-element.1756, ...), kind=kOutput, calls=%fused_computation.41.clone.1 | convolution fusion | flops 395182080 | bytes 902144 | tf_op jit(solution)/shard_map/while/body/eval_jaxpr/dot_general | solution.py:72
  131.4 4.6 %fusion.190 = f32[80,1,4096]{2,0,1:T(8,128)S(1)} fusion(f32[80,1,4096]{2,0,1:T(8,128)S(1)} %get-tuple-element.1733, s32[]{:T(128)S(6)} %select_n.596, bf16[80,1152]{1,0:T(8,128)(2,1)} %get-tuple-element.1757, bf16[80,1152]{1,0:T(8,128)(2,1)} %get-tuple-element.1750, f32[1152]{0:T(1024)S(1)} %get-tuple-element.1756, ...), kind=kOutput, calls=%fused_computation.41.clone.1 | convolution fusion | flops 395182080 | bytes 902144 | tf_op jit(solution)/shard_map/while/body/eval_jaxpr/dot_general | solution.py:72
  136.1 4.6 %fusion.190 = f32[80,1,4096]{2,0,1:T(8,128)S(1)} fusion(f32[80,1,4096]{2,0,1:T(8,128)S(1)} %get-tuple-element.1733, s32[]{:T(128)S(6)} %select_n.596, bf16[80,1152]{1,0:T(8,128)(2,1)} %get-tuple-element.1757, bf16[80,1152]{1,0:T(8,128)(2,1)} %get-tuple-element.1750, f32[1152]{0:T(1024)S(1)} %get-tuple-element.1756, ...), kind=kOutput, calls=%fused_computation.41.clone.1 | convolution fusion | flops 395182080 | bytes 902144 | tf_op jit(solution)/shard_map/while/body/eval_jaxpr/dot_general | solution.py:72
  142.6 3.4 %fusion.146 = (f32[4096]{0:T(1024)S(1)}, f32[80,1,4096]{0,2,1:T(8,128)}) fusion(f32[80,1,4096]{0,2,1:T(8,128)S(1)} %get-tuple-element.1265, f32[80,1,4096]{0,2,1:T(8,128)} %copy.36), kind=kLoop, calls=%fused_computation.311 | loop fusion | flops 651264 | bytes 3948544 | tf_op jit(solution)/shard_map/reduce_sum | solution.py:40
  146.0 2.4 gather_fusion.2
  150.9 2.4 %collective-permute-start.17 = (bf16[2,80,128]{1,2,0:T(8,128)(2,1)S(1)}, bf16[2,80,128]{1,2,0:T(8,128)(2,1)S(1)}, u32[]{:S(2)}, u32[]{:S(2)}) collective-permute-start(bf16[2,80,128]{1,2,0:T(8,128)(2,1)S(1)} %get-tuple-element.1303), channel_id=1, source_target_pairs={{4,0},{8,4},{12,8},{16,12},{20,16},{24,20},{28,24},{5,1},{9,5},{13... | collective-permute-start | bytes 122888 | tf_op jit(solution)/shard_map/ppermute | solution.py:12
  153.4 3.1 %collective-permute-done.17 = bf16[2,80,128]{1,2,0:T(8,128)(2,1)S(1)} collective-permute-done((bf16[2,80,128]{1,2,0:T(8,128)(2,1)S(1)}, bf16[2,80,128]{1,2,0:T(8,128)(2,1)S(1)}, u32[]{:S(2)}, u32[]{:S(2)}) %collective-permute-start.17) | collective-permute-done | bytes 40992 | tf_op jit(solution)/shard_map/ppermute | solution.py:12
  156.6 2.5 %collective-permute-start.18 = (bf16[3,2,80,128]{2,3,1,0:T(8,128)(2,1)S(1)}, bf16[3,2,80,128]{2,3,1,0:T(8,128)(2,1)S(1)}, u32[]{:S(2)}, u32[]{:S(2)}) collective-permute-start(bf16[3,2,80,128]{2,3,1,0:T(8,128)(2,1)S(1)} %get-tuple-element.1287), channel_id=1, source_target_pairs={{0,1},{1,2},{2,3},{3,0},{4,5},{5,6},{6,7},{7,4},{8,9},{9,10},{10,1... | collective-permute-start | bytes 368648 | tf_op jit(solution)/shard_map/ppermute | solution.py:18
  161.6 2.1 collective-permute-done.18
  163.7 4.2 %collective-permute-done.19 = bf16[3,2,80,128]{2,3,1,0:T(8,128)(2,1)S(1)} collective-permute-done((bf16[3,2,80,128]{2,3,1,0:T(8,128)(2,1)S(1)}, bf16[3,2,80,128]{2,3,1,0:T(8,128)(2,1)S(1)}, u32[]{:S(2)}, u32[]{:S(2)}) %collective-permute-start.19) | collective-permute-done | bytes 122912 | tf_op jit(solution)/shard_map/ppermute | solution.py:18
  168.7 14.6 %while.62 = (s32[]{:T(128)}, f32[80,1,4096]{2,0,1:T(8,128)S(1)}, bf16[80,1,4096]{2,0,1:T(8,128)(2,1)S(1)}, bf16[80,1152]{1,0:T(8,128)(2,1)S(1)}, s32[]{:T(128)},...) while((s32[]{:T(128)}, f32[80,1,4096]{2,0,1:T(8,128)S(1)}, ...), condition=%wide.region_14.16_spmd, body=%wide.region_13.15_spmd.sunk | while | flops 395204608 | bytes 928975 | solution.py:79
  168.8 3.6 %fusion.195 = f32[80,1,4096]{2,0,1:T(8,128)S(1)} fusion(f32[80,1,4096]{2,0,1:T(8,128)S(1)} %get-tuple-element.1778, s32[]{:T(128)S(6)} %select_n.599, bf16[80,1152]{1,0:T(8,128)(2,1)S(1)} %get-tuple-element.1802, bf16[80,1152]{1,0:T(8,128)(2,1)S(1)} %get-tuple-element.1795, f32[1152]{0:T(1024)S(1)} %get-tuple-element.1801, ...), kind=kOutput, calls=%fused_computation.70.clone.1 | convolution fusion | flops 395182080 | bytes 902144 | tf_op jit(solution)/shard_map/while/body/eval_jaxpr/dot_general | solution.py:72
  172.4 3.6 %fusion.195 = f32[80,1,4096]{2,0,1:T(8,128)S(1)} fusion(f32[80,1,4096]{2,0,1:T(8,128)S(1)} %get-tuple-element.1778, s32[]{:T(128)S(6)} %select_n.599, bf16[80,1152]{1,0:T(8,128)(2,1)S(1)} %get-tuple-element.1802, bf16[80,1152]{1,0:T(8,128)(2,1)S(1)} %get-tuple-element.1795, f32[1152]{0:T(1024)S(1)} %get-tuple-element.1801, ...), kind=kOutput, calls=%fused_computation.70.clone.1 | convolution fusion | flops 395182080 | bytes 902144 | tf_op jit(solution)/shard_map/while/body/eval_jaxpr/dot_general | solution.py:72
  176.1 3.6 %fusion.195 = f32[80,1,4096]{2,0,1:T(8,128)S(1)} fusion(f32[80,1,4096]{2,0,1:T(8,128)S(1)} %get-tuple-element.1778, s32[]{:T(128)S(6)} %select_n.599, bf16[80,1152]{1,0:T(8,128)(2,1)S(1)} %get-tuple-element.1802, bf16[80,1152]{1,0:T(8,128)(2,1)S(1)} %get-tuple-element.1795, f32[1152]{0:T(1024)S(1)} %get-tuple-element.1801, ...), kind=kOutput, calls=%fused_computation.70.clone.1 | convolution fusion | flops 395182080 | bytes 902144 | tf_op jit(solution)/shard_map/while/body/eval_jaxpr/dot_general | solution.py:72
  179.7 3.6 %fusion.195 = f32[80,1,4096]{2,0,1:T(8,128)S(1)} fusion(f32[80,1,4096]{2,0,1:T(8,128)S(1)} %get-tuple-element.1778, s32[]{:T(128)S(6)} %select_n.599, bf16[80,1152]{1,0:T(8,128)(2,1)S(1)} %get-tuple-element.1802, bf16[80,1152]{1,0:T(8,128)(2,1)S(1)} %get-tuple-element.1795, f32[1152]{0:T(1024)S(1)} %get-tuple-element.1801, ...), kind=kOutput, calls=%fused_computation.70.clone.1 | convolution fusion | flops 395182080 | bytes 902144 | tf_op jit(solution)/shard_map/while/body/eval_jaxpr/dot_general | solution.py:72
  185.1 2.8 %fusion.145 = (f32[4096]{0:T(1024)S(1)}, f32[80,1,4096]{0,2,1:T(8,128)S(1)}) fusion(f32[80,1,4096]{0,2,1:T(8,128)} %get-tuple-element.1261, f32[80,1,4096]{0,2,1:T(8,128)} %copy.40), kind=kLoop, calls=%fused_computation.310 | loop fusion | flops 651264 | bytes 3948544 | tf_op jit(solution)/shard_map/reduce_sum | solution.py:40
  191.2 3.0 %collective-permute-start.25 = (bf16[2,80,128]{1,2,0:T(8,128)(2,1)S(1)}, bf16[2,80,128]{1,2,0:T(8,128)(2,1)S(1)}, u32[]{:S(2)}, u32[]{:S(2)}) collective-permute-start(bf16[2,80,128]{1,2,0:T(8,128)(2,1)S(1)} %get-tuple-element.1301), channel_id=1, source_target_pairs={{4,0},{8,4},{12,8},{16,12},{20,16},{24,20},{28,24},{5,1},{9,5},{13... | collective-permute-start | bytes 122888 | tf_op jit(solution)/shard_map/ppermute | solution.py:12
  194.3 2.5 %collective-permute-done.25 = bf16[2,80,128]{1,2,0:T(8,128)(2,1)S(1)} collective-permute-done((bf16[2,80,128]{1,2,0:T(8,128)(2,1)S(1)}, bf16[2,80,128]{1,2,0:T(8,128)(2,1)S(1)}, u32[]{:S(2)}, u32[]{:S(2)}) %collective-permute-start.25) | collective-permute-done | bytes 40992 | tf_op jit(solution)/shard_map/ppermute | solution.py:12
  201.8 2.1 collective-permute-done.26
  204.0 3.5 %collective-permute-done.27 = bf16[3,2,80,128]{2,3,1,0:T(8,128)(2,1)} collective-permute-done((bf16[3,2,80,128]{2,3,1,0:T(8,128)(2,1)}, bf16[3,2,80,128]{2,3,1,0:T(8,128)(2,1)}, u32[]{:S(2)}, u32[]{:S(2)}) %collective-permute-start.27) | collective-permute-done | bytes 122912 | tf_op jit(solution)/shard_map/ppermute | solution.py:18
  210.4 18.9 %while.63 = (s32[]{:T(128)}, f32[80,1,4096]{2,0,1:T(8,128)S(1)}, bf16[80,1,4096]{2,0,1:T(8,128)(2,1)}, bf16[80,1152]{1,0:T(8,128)(2,1)}, s32[]{:T(128)}, /*index...) while((s32[]{:T(128)}, f32[80,1,4096]{2,0,1:T(8,128)S(1)}, ...), condition=%wide.region_19.21_spmd, body=%wide.region_18.20_spmd.sunk | while | flops 395204608 | bytes 928975 | solution.py:79
  210.5 4.6 %fusion.200 = f32[80,1,4096]{2,0,1:T(8,128)S(1)} fusion(f32[80,1,4096]{2,0,1:T(8,128)S(1)} %get-tuple-element.1823, s32[]{:T(128)S(6)} %select_n.602, bf16[80,1152]{1,0:T(8,128)(2,1)} %get-tuple-element.1847, bf16[80,1152]{1,0:T(8,128)(2,1)} %get-tuple-element.1840, f32[1152]{0:T(1024)S(1)} %get-tuple-element.1846, ...), kind=kOutput, calls=%fused_computation.99.clone.1 | convolution fusion | flops 395182080 | bytes 902144 | tf_op jit(solution)/shard_map/while/body/eval_jaxpr/dot_general | solution.py:72
  215.2 4.6 %fusion.200 = f32[80,1,4096]{2,0,1:T(8,128)S(1)} fusion(f32[80,1,4096]{2,0,1:T(8,128)S(1)} %get-tuple-element.1823, s32[]{:T(128)S(6)} %select_n.602, bf16[80,1152]{1,0:T(8,128)(2,1)} %get-tuple-element.1847, bf16[80,1152]{1,0:T(8,128)(2,1)} %get-tuple-element.1840, f32[1152]{0:T(1024)S(1)} %get-tuple-element.1846, ...), kind=kOutput, calls=%fused_computation.99.clone.1 | convolution fusion | flops 395182080 | bytes 902144 | tf_op jit(solution)/shard_map/while/body/eval_jaxpr/dot_general | solution.py:72
  220.0 4.6 %fusion.200 = f32[80,1,4096]{2,0,1:T(8,128)S(1)} fusion(f32[80,1,4096]{2,0,1:T(8,128)S(1)} %get-tuple-element.1823, s32[]{:T(128)S(6)} %select_n.602, bf16[80,1152]{1,0:T(8,128)(2,1)} %get-tuple-element.1847, bf16[80,1152]{1,0:T(8,128)(2,1)} %get-tuple-element.1840, f32[1152]{0:T(1024)S(1)} %get-tuple-element.1846, ...), kind=kOutput, calls=%fused_computation.99.clone.1 | convolution fusion | flops 395182080 | bytes 902144 | tf_op jit(solution)/shard_map/while/body/eval_jaxpr/dot_general | solution.py:72
  224.7 4.6 %fusion.200 = f32[80,1,4096]{2,0,1:T(8,128)S(1)} fusion(f32[80,1,4096]{2,0,1:T(8,128)S(1)} %get-tuple-element.1823, s32[]{:T(128)S(6)} %select_n.602, bf16[80,1152]{1,0:T(8,128)(2,1)} %get-tuple-element.1847, bf16[80,1152]{1,0:T(8,128)(2,1)} %get-tuple-element.1840, f32[1152]{0:T(1024)S(1)} %get-tuple-element.1846, ...), kind=kOutput, calls=%fused_computation.99.clone.1 | convolution fusion | flops 395182080 | bytes 902144 | tf_op jit(solution)/shard_map/while/body/eval_jaxpr/dot_general | solution.py:72
  231.1 3.2 %add.839 = f32[80,1,4096]{0,2,1:T(8,128)} add(f32[80,1,4096]{0,2,1:T(8,128)S(1)} %get-tuple-element.1257, f32[80,1,4096]{0,2,1:T(8,128)} %copy.44) | non-fusion elementwise | flops 327680 | bytes 3932160 | tf_op jit(solution)/shard_map/add | solution.py:80
  234.3 2.8 %copy.45 = f32[80,1,32,128]{3,2,1,0:T(8,128)} copy(f32[80,1,32,128]{0,3,2,1:T(8,128)} %bitcast.421) | data formatting | bytes 2621440 | tf_op jit(solution)/shard_map/reshape | solution.py:80
  (242 shorter events, 75.8 us)
Async XLA Ops:
  0.0 11.4 %copy-start.19 = (s32[4,1,1,128]{3,2,1,0:T(1,128)S(1)}, s32[4,1,1,128]{3,2,1,0:T(1,128)}, u32[]{:S(2)}) copy-start(s32[4,1,1,128]{3,2,1,0:T(1,128)} %param.20) | copy-start | bytes 6148
  0.0 14.2 %copy-start.15 = (s32[4,1,1]{0,2,1:T(1,128)S(1)}, s32[4,1,1]{0,2,1:T(1,128)}, u32[]{:S(2)}) copy-start(s32[4,1,1]{0,2,1:T(1,128)} %param.22) | copy-start | bytes 52
  6.8 16.0 %copy-start.20 = (s32[4,1,1,128]{3,2,1,0:T(1,128)S(1)}, s32[4,1,1,128]{3,2,1,0:T(1,128)}, u32[]{:S(2)}) copy-start(s32[4,1,1,128]{3,2,1,0:T(1,128)} %param.21) | copy-start | bytes 6148
  6.8 25.3 %copy-start.1 = (f32[80,1,32,128]{3,2,1,0:T(8,128)S(1)}, f32[80,1,32,128]{3,2,1,0:T(8,128)}, u32[]{:S(2)}) copy-start(f32[80,1,32,128]{3,2,1,0:T(8,128)} %param.17) | copy-start | bytes 3932164
  8.7 24.4 %copy-start = (f32[80,1,32,128]{0,3,2,1:T(8,128)}, f32[80,1,32,128]{0,3,2,1:T(8,128)S(1)}, u32[]{:S(2)}) copy-start(f32[80,1,32,128]{0,3,2,1:T(8,128)S(1)} %copy.27) | copy-start | bytes 3932164
  17.1 45.9 %collective-permute-start = (bf16[2,80,128]{1,2,0:T(8,128)(2,1)}, bf16[2,80,128]{1,2,0:T(8,128)(2,1)}, u32[]{:S(2)}, u32[]{:S(2)}) collective-permute-start(bf16[2,80,128]{1,2,0:T(8,128)(2,1)} %get-tuple-element.1307), channel_id=1, source_target_pairs={{0,4},{4,8},{8,12},{12,16},{16,20},{20,24},{24,28},{1,5},{5,9},{9,... | collective-permute-start | bytes 122888 | tf_op jit(solution)/shard_map/ppermute | solution.py:12
  20.8 42.2 %collective-permute-start.1 = (bf16[2,80,128]{1,2,0:T(8,128)(2,1)}, bf16[2,80,128]{1,2,0:T(8,128)(2,1)}, u32[]{:S(2)}, u32[]{:S(2)}) collective-permute-start(bf16[2,80,128]{1,2,0:T(8,128)(2,1)} %get-tuple-element.1307), channel_id=1, source_target_pairs={{4,0},{8,4},{12,8},{16,12},{20,16},{24,20},{28,24},{5,1},{9,5},{13... | collective-permute-start | bytes 122888 | tf_op jit(solution)/shard_map/ppermute | solution.py:12
  22.9 14.4 %collective-permute-start.4 = (s32[3,128]{1,0:T(4,128)S(1)}, s32[3,128]{1,0:T(4,128)S(1)}, u32[]{:S(2)}, u32[]{:S(2)}) collective-permute-start(s32[3,128]{1,0:T(4,128)S(1)} %get-tuple-element.1361), channel_id=1, source_target_pairs={{0,4},{4,8},{8,12},{12,16},{16,20},{20,24},{24,28},{1,5},{5,9},{9,... | collective-permute-start | bytes 4616 | tf_op jit(solution)/shard_map/ppermute | solution.py:12
  26.5 12.7 %collective-permute-start.5 = (s32[3,128]{1,0:T(4,128)S(1)}, s32[3,128]{1,0:T(4,128)S(1)}, u32[]{:S(2)}, u32[]{:S(2)}) collective-permute-start(s32[3,128]{1,0:T(4,128)S(1)} %get-tuple-element.1361), channel_id=1, source_target_pairs={{4,0},{8,4},{12,8},{16,12},{20,16},{24,20},{28,24},{5,1},{9,5},{13... | collective-permute-start | bytes 4616 | tf_op jit(solution)/shard_map/ppermute | solution.py:12
  28.5 13.3 %collective-permute-start.12 = (s32[3,128]{1,0:T(4,128)S(1)}, s32[3,128]{1,0:T(4,128)S(1)}, u32[]{:S(2)}, u32[]{:S(2)}) collective-permute-start(s32[3,128]{1,0:T(4,128)S(1)} %get-tuple-element.1359), channel_id=1, source_target_pairs={{0,4},{4,8},{8,12},{12,16},{16,20},{20,24},{24,28},{1,5},{5,9},{9,... | collective-permute-start | bytes 4616 | tf_op jit(solution)/shard_map/ppermute | solution.py:12
  37.3 7.5 %collective-permute-start.13 = (s32[3,128]{1,0:T(4,128)S(1)}, s32[3,128]{1,0:T(4,128)S(1)}, u32[]{:S(2)}, u32[]{:S(2)}) collective-permute-start(s32[3,128]{1,0:T(4,128)S(1)} %get-tuple-element.1359), channel_id=1, source_target_pairs={{4,0},{8,4},{12,8},{16,12},{20,16},{24,20},{28,24},{5,1},{9,5},{13... | collective-permute-start | bytes 4616 | tf_op jit(solution)/shard_map/ppermute | solution.py:12
  39.2 8.0 %collective-permute-start.21 = (s32[3,128]{1,0:T(4,128)S(1)}, s32[3,128]{1,0:T(4,128)S(1)}, u32[]{:S(2)}, u32[]{:S(2)}) collective-permute-start(s32[3,128]{1,0:T(4,128)S(1)} %get-tuple-element.1357), channel_id=1, source_target_pairs={{4,0},{8,4},{12,8},{16,12},{20,16},{24,20},{28,24},{5,1},{9,5},{13... | collective-permute-start | bytes 4616 | tf_op jit(solution)/shard_map/ppermute | solution.py:12
  41.7 7.5 %collective-permute-start.20 = (s32[3,128]{1,0:T(4,128)S(1)}, s32[3,128]{1,0:T(4,128)S(1)}, u32[]{:S(2)}, u32[]{:S(2)}) collective-permute-start(s32[3,128]{1,0:T(4,128)S(1)} %get-tuple-element.1357), channel_id=1, source_target_pairs={{0,4},{4,8},{8,12},{12,16},{16,20},{20,24},{24,28},{1,5},{5,9},{9,... | collective-permute-start | bytes 4616 | tf_op jit(solution)/shard_map/ppermute | solution.py:12
  44.9 5.6 %collective-permute-start.28 = (s32[3,128]{1,0:T(4,128)S(1)}, s32[3,128]{1,0:T(4,128)S(1)}, u32[]{:S(2)}, u32[]{:S(2)}) collective-permute-start(s32[3,128]{1,0:T(4,128)S(1)} %get-tuple-element.1355), channel_id=1, source_target_pairs={{0,4},{4,8},{8,12},{12,16},{16,20},{20,24},{24,28},{1,5},{5,9},{9,... | collective-permute-start | bytes 4616 | tf_op jit(solution)/shard_map/ppermute | solution.py:12
  47.3 4.9 %collective-permute-start.29 = (s32[3,128]{1,0:T(4,128)S(1)}, s32[3,128]{1,0:T(4,128)S(1)}, u32[]{:S(2)}, u32[]{:S(2)}) collective-permute-start(s32[3,128]{1,0:T(4,128)S(1)} %get-tuple-element.1355), channel_id=1, source_target_pairs={{4,0},{8,4},{12,8},{16,12},{20,16},{24,20},{28,24},{5,1},{9,5},{13... | collective-permute-start | bytes 4616 | tf_op jit(solution)/shard_map/ppermute | solution.py:12
  49.2 4.2 %collective-permute-start.6 = (s32[3,3,128]{2,1,0:T(4,128)S(1)}, s32[3,3,128]{2,1,0:T(4,128)S(1)}, u32[]{:S(2)}, u32[]{:S(2)}) collective-permute-start(s32[3,3,128]{2,1,0:T(4,128)S(1)} %get-tuple-element.1327), channel_id=1, source_target_pairs={{0,1},{1,2},{2,3},{3,0},{4,5},{5,6},{6,7},{7,4},{8,9},{9,10},{10,1... | collective-permute-start | bytes 13832 | tf_op jit(solution)/shard_map/ppermute | solution.py:18
  50.5 4.1 %collective-permute-start.7 = (s32[3,3,128]{2,1,0:T(4,128)S(1)}, s32[3,3,128]{2,1,0:T(4,128)S(1)}, u32[]{:S(2)}, u32[]{:S(2)}) collective-permute-start(s32[3,3,128]{2,1,0:T(4,128)S(1)} %get-tuple-element.1327), channel_id=1, source_target_pairs={{0,3},{1,0},{2,1},{3,2},{4,7},{5,4},{6,5},{7,6},{8,11},{9,8},{10,9... | collective-permute-start | bytes 13832 | tf_op jit(solution)/shard_map/ppermute | solution.py:18
  52.2 3.4 %collective-permute-start.14 = (s32[3,3,128]{2,1,0:T(4,128)S(1)}, s32[3,3,128]{2,1,0:T(4,128)S(1)}, u32[]{:S(2)}, u32[]{:S(2)}) collective-permute-start(s32[3,3,128]{2,1,0:T(4,128)S(1)} %get-tuple-element.1325), channel_id=1, source_target_pairs={{0,1},{1,2},{2,3},{3,0},{4,5},{5,6},{6,7},{7,4},{8,9},{9,10},{10,1... | collective-permute-start | bytes 13832 | tf_op jit(solution)/shard_map/ppermute | solution.py:18
  53.4 3.6 %collective-permute-start.15 = (s32[3,3,128]{2,1,0:T(4,128)S(1)}, s32[3,3,128]{2,1,0:T(4,128)S(1)}, u32[]{:S(2)}, u32[]{:S(2)}) collective-permute-start(s32[3,3,128]{2,1,0:T(4,128)S(1)} %get-tuple-element.1325), channel_id=1, source_target_pairs={{0,3},{1,0},{2,1},{3,2},{4,7},{5,4},{6,5},{7,6},{8,11},{9,8},{10,9... | collective-permute-start | bytes 13832 | tf_op jit(solution)/shard_map/ppermute | solution.py:18
  54.6 4.7 %collective-permute-start.22 = (s32[3,3,128]{2,1,0:T(4,128)S(1)}, s32[3,3,128]{2,1,0:T(4,128)S(1)}, u32[]{:S(2)}, u32[]{:S(2)}) collective-permute-start(s32[3,3,128]{2,1,0:T(4,128)S(1)} %get-tuple-element.1323), channel_id=1, source_target_pairs={{0,1},{1,2},{2,3},{3,0},{4,5},{5,6},{6,7},{7,4},{8,9},{9,10},{10,1... | collective-permute-start | bytes 13832 | tf_op jit(solution)/shard_map/ppermute | solution.py:18
  55.6 5.1 %collective-permute-start.23 = (s32[3,3,128]{2,1,0:T(4,128)S(1)}, s32[3,3,128]{2,1,0:T(4,128)S(1)}, u32[]{:S(2)}, u32[]{:S(2)}) collective-permute-start(s32[3,3,128]{2,1,0:T(4,128)S(1)} %get-tuple-element.1323), channel_id=1, source_target_pairs={{0,3},{1,0},{2,1},{3,2},{4,7},{5,4},{6,5},{7,6},{8,11},{9,8},{10,9... | collective-permute-start | bytes 13832 | tf_op jit(solution)/shard_map/ppermute | solution.py:18
  57.0 3.6 %collective-permute-start.30 = (s32[3,3,128]{2,1,0:T(4,128)S(1)}, s32[3,3,128]{2,1,0:T(4,128)S(1)}, u32[]{:S(2)}, u32[]{:S(2)}) collective-permute-start(s32[3,3,128]{2,1,0:T(4,128)S(1)} %get-tuple-element.1321), channel_id=1, source_target_pairs={{0,1},{1,2},{2,3},{3,0},{4,5},{5,6},{6,7},{7,4},{8,9},{9,10},{10,1... | collective-permute-start | bytes 13832 | tf_op jit(solution)/shard_map/ppermute | solution.py:18
  58.7 13.9 %copy-start.10 = (s32[1152]{0:T(1024)}, s32[1152]{0:T(1024)S(1)}, u32[]{:S(2)}) copy-start(s32[1152]{0:T(1024)S(1)} %mul.355) | copy-start | bytes 13828
  59.3 2.5 %collective-permute-start.31 = (s32[3,3,128]{2,1,0:T(4,128)S(1)}, s32[3,3,128]{2,1,0:T(4,128)S(1)}, u32[]{:S(2)}, u32[]{:S(2)}) collective-permute-start(s32[3,3,128]{2,1,0:T(4,128)S(1)} %get-tuple-element.1321), channel_id=1, source_target_pairs={{0,3},{1,0},{2,1},{3,2},{4,7},{5,4},{6,5},{7,6},{8,11},{9,8},{10,9... | collective-permute-start | bytes 13832 | tf_op jit(solution)/shard_map/ppermute | solution.py:18
  63.0 10.3 %copy-start.6 = (s32[1152]{0:T(1024)}, s32[1152]{0:T(1024)S(1)}, u32[]{:S(2)}) copy-start(s32[1152]{0:T(1024)S(1)} %mul.371) | copy-start | bytes 13828
  63.9 5.5 %collective-permute-start.2 = (bf16[3,2,80,128]{2,3,1,0:T(8,128)(2,1)S(1)}, bf16[3,2,80,128]{2,3,1,0:T(8,128)(2,1)S(1)}, u32[]{:S(2)}, u32[]{:S(2)}) collective-permute-start(bf16[3,2,80,128]{2,3,1,0:T(8,128)(2,1)S(1)} %get-tuple-element.1291), channel_id=1, source_target_pairs={{0,1},{1,2},{2,3},{3,0},{4,5},{5,6},{6,7},{7,4},{8,9},{9,10},{10,1... | collective-permute-start | bytes 368648 | tf_op jit(solution)/shard_map/ppermute | solution.py:18
  66.3 6.3 %collective-permute-start.3 = (bf16[3,2,80,128]{2,3,1,0:T(8,128)(2,1)S(1)}, bf16[3,2,80,128]{2,3,1,0:T(8,128)(2,1)S(1)}, u32[]{:S(2)}, u32[]{:S(2)}) collective-permute-start(bf16[3,2,80,128]{2,3,1,0:T(8,128)(2,1)S(1)} %get-tuple-element.1291), channel_id=1, source_target_pairs={{0,3},{1,0},{2,1},{3,2},{4,7},{5,4},{6,5},{7,6},{8,11},{9,8},{10,9... | collective-permute-start | bytes 368648 | tf_op jit(solution)/shard_map/ppermute | solution.py:18
  89.7 3.6 %copy-start.14 = (pred[128]{0:T(512)(128)(4,1)S(1)}, pred[128]{0:T(512)(128)(4,1)}, u32[]{:S(2)}) copy-start(pred[128]{0:T(512)(128)(4,1)} %get-tuple-element.1348) | copy-start | bytes 388
  95.2 7.9 %collective-permute-start.8 = (bf16[2,80,128]{1,2,0:T(8,128)(2,1)S(1)}, bf16[2,80,128]{1,2,0:T(8,128)(2,1)S(1)}, u32[]{:S(2)}, u32[]{:S(2)}) collective-permute-start(bf16[2,80,128]{1,2,0:T(8,128)(2,1)S(1)} %get-tuple-element.1305), channel_id=1, source_target_pairs={{0,4},{4,8},{8,12},{12,16},{16,20},{20,24},{24,28},{1,5},{5,9},{9,... | collective-permute-start | bytes 122888 | tf_op jit(solution)/shard_map/ppermute | solution.py:12
  101.2 5.6 %collective-permute-start.9 = (bf16[2,80,128]{1,2,0:T(8,128)(2,1)S(1)}, bf16[2,80,128]{1,2,0:T(8,128)(2,1)S(1)}, u32[]{:S(2)}, u32[]{:S(2)}) collective-permute-start(bf16[2,80,128]{1,2,0:T(8,128)(2,1)S(1)} %get-tuple-element.1305), channel_id=1, source_target_pairs={{4,0},{8,4},{12,8},{16,12},{20,16},{24,20},{28,24},{5,1},{9,5},{13... | collective-permute-start | bytes 122888 | tf_op jit(solution)/shard_map/ppermute | solution.py:12
  107.5 8.0 %collective-permute-start.10 = (bf16[3,2,80,128]{2,3,1,0:T(8,128)(2,1)}, bf16[3,2,80,128]{2,3,1,0:T(8,128)(2,1)S(1)}, u32[]{:S(2)}, u32[]{:S(2)}) collective-permute-start(bf16[3,2,80,128]{2,3,1,0:T(8,128)(2,1)} %get-tuple-element.1289), channel_id=1, source_target_pairs={{0,1},{1,2},{2,3},{3,0},{4,5},{5,6},{6,7},{7,4},{8,9},{9,10},{10,1... | collective-permute-start | bytes 368648 | tf_op jit(solution)/shard_map/ppermute | solution.py:18
  109.4 9.5 %collective-permute-start.11 = (bf16[3,2,80,128]{2,3,1,0:T(8,128)(2,1)}, bf16[3,2,80,128]{2,3,1,0:T(8,128)(2,1)}, u32[]{:S(2)}, u32[]{:S(2)}) collective-permute-start(bf16[3,2,80,128]{2,3,1,0:T(8,128)(2,1)} %get-tuple-element.1289), channel_id=1, source_target_pairs={{0,3},{1,0},{2,1},{3,2},{4,7},{5,4},{6,5},{7,6},{8,11},{9,8},{10,9... | collective-permute-start | bytes 368648 | tf_op jit(solution)/shard_map/ppermute | solution.py:18
  142.6 5.8 %copy-start.13 = (pred[128]{0:T(512)(128)(4,1)S(1)}, pred[128]{0:T(512)(128)(4,1)}, u32[]{:S(2)}) copy-start(pred[128]{0:T(512)(128)(4,1)} %get-tuple-element.1352) | copy-start | bytes 388
  142.6 6.0 %copy-start.21 = (f32[4,1,1,128]{3,2,1,0:T(1,128)S(1)}, f32[4,1,1,128]{3,2,1,0:T(1,128)}, u32[]{:S(2)}) copy-start(f32[4,1,1,128]{3,2,1,0:T(1,128)} %param.18) | copy-start | bytes 6148
  142.6 6.2 %copy-start.22 = (f32[4,1,1,128]{3,2,1,0:T(1,128)S(1)}, f32[4,1,1,128]{3,2,1,0:T(1,128)}, u32[]{:S(2)}) copy-start(f32[4,1,1,128]{3,2,1,0:T(1,128)} %param.19) | copy-start | bytes 6148
  142.6 6.2 %copy-start.24 = (pred[128]{0:T(512)(128)(4,1)S(1)}, pred[128]{0:T(512)(128)(4,1)}, u32[]{:S(2)}) copy-start(pred[128]{0:T(512)(128)(4,1)} %iota_compare_fusion.1) | copy-start | bytes 388
  149.0 4.4 %collective-permute-start.16 = (bf16[2,80,128]{1,2,0:T(8,128)(2,1)S(1)}, bf16[2,80,128]{1,2,0:T(8,128)(2,1)S(1)}, u32[]{:S(2)}, u32[]{:S(2)}) collective-permute-start(bf16[2,80,128]{1,2,0:T(8,128)(2,1)S(1)} %get-tuple-element.1303), channel_id=1, source_target_pairs={{0,4},{4,8},{8,12},{12,16},{16,20},{20,24},{24,28},{1,5},{5,9},{9,... | collective-permute-start | bytes 122888 | tf_op jit(solution)/shard_map/ppermute | solution.py:12
  150.9 5.6 %collective-permute-start.17 = (bf16[2,80,128]{1,2,0:T(8,128)(2,1)S(1)}, bf16[2,80,128]{1,2,0:T(8,128)(2,1)S(1)}, u32[]{:S(2)}, u32[]{:S(2)}) collective-permute-start(bf16[2,80,128]{1,2,0:T(8,128)(2,1)S(1)} %get-tuple-element.1303), channel_id=1, source_target_pairs={{4,0},{8,4},{12,8},{16,12},{20,16},{24,20},{28,24},{5,1},{9,5},{13... | collective-permute-start | bytes 122888 | tf_op jit(solution)/shard_map/ppermute | solution.py:12
  156.6 7.2 %collective-permute-start.18 = (bf16[3,2,80,128]{2,3,1,0:T(8,128)(2,1)S(1)}, bf16[3,2,80,128]{2,3,1,0:T(8,128)(2,1)S(1)}, u32[]{:S(2)}, u32[]{:S(2)}) collective-permute-start(bf16[3,2,80,128]{2,3,1,0:T(8,128)(2,1)S(1)} %get-tuple-element.1287), channel_id=1, source_target_pairs={{0,1},{1,2},{2,3},{3,0},{4,5},{5,6},{6,7},{7,4},{8,9},{9,10},{10,1... | collective-permute-start | bytes 368648 | tf_op jit(solution)/shard_map/ppermute | solution.py:18
  159.1 8.9 %collective-permute-start.19 = (bf16[3,2,80,128]{2,3,1,0:T(8,128)(2,1)S(1)}, bf16[3,2,80,128]{2,3,1,0:T(8,128)(2,1)S(1)}, u32[]{:S(2)}, u32[]{:S(2)}) collective-permute-start(bf16[3,2,80,128]{2,3,1,0:T(8,128)(2,1)S(1)} %get-tuple-element.1287), channel_id=1, source_target_pairs={{0,3},{1,0},{2,1},{3,2},{4,7},{5,4},{6,5},{7,6},{8,11},{9,8},{10,9... | collective-permute-start | bytes 368648 | tf_op jit(solution)/shard_map/ppermute | solution.py:18
  185.1 3.6 %copy-start.12 = (pred[128]{0:T(512)(128)(4,1)S(1)}, pred[128]{0:T(512)(128)(4,1)}, u32[]{:S(2)}) copy-start(pred[128]{0:T(512)(128)(4,1)} %get-tuple-element.1254) | copy-start | bytes 388
  185.1 4.0 %copy-start.23 = (pred[128]{0:T(512)(128)(4,1)S(1)}, pred[128]{0:T(512)(128)(4,1)}, u32[]{:S(2)}) copy-start(pred[128]{0:T(512)(128)(4,1)} %iota_compare_fusion) | copy-start | bytes 388
  189.3 5.0 %collective-permute-start.24 = (bf16[2,80,128]{1,2,0:T(8,128)(2,1)S(1)}, bf16[2,80,128]{1,2,0:T(8,128)(2,1)S(1)}, u32[]{:S(2)}, u32[]{:S(2)}) collective-permute-start(bf16[2,80,128]{1,2,0:T(8,128)(2,1)S(1)} %get-tuple-element.1301), channel_id=1, source_target_pairs={{0,4},{4,8},{8,12},{12,16},{16,20},{20,24},{24,28},{1,5},{5,9},{9,... | collective-permute-start | bytes 122888 | tf_op jit(solution)/shard_map/ppermute | solution.py:12
  191.2 5.6 %collective-permute-start.25 = (bf16[2,80,128]{1,2,0:T(8,128)(2,1)S(1)}, bf16[2,80,128]{1,2,0:T(8,128)(2,1)S(1)}, u32[]{:S(2)}, u32[]{:S(2)}) collective-permute-start(bf16[2,80,128]{1,2,0:T(8,128)(2,1)S(1)} %get-tuple-element.1301), channel_id=1, source_target_pairs={{4,0},{8,4},{12,8},{16,12},{20,16},{24,20},{28,24},{5,1},{9,5},{13... | collective-permute-start | bytes 122888 | tf_op jit(solution)/shard_map/ppermute | solution.py:12
  197.5 6.4 %collective-permute-start.26 = (bf16[3,2,80,128]{2,3,1,0:T(8,128)(2,1)}, bf16[3,2,80,128]{2,3,1,0:T(8,128)(2,1)S(1)}, u32[]{:S(2)}, u32[]{:S(2)}) collective-permute-start(bf16[3,2,80,128]{2,3,1,0:T(8,128)(2,1)} %get-tuple-element.1285), channel_id=1, source_target_pairs={{0,1},{1,2},{2,3},{3,0},{4,5},{5,6},{6,7},{7,4},{8,9},{9,10},{10,1... | collective-permute-start | bytes 368648 | tf_op jit(solution)/shard_map/ppermute | solution.py:18
  198.8 8.6 %collective-permute-start.27 = (bf16[3,2,80,128]{2,3,1,0:T(8,128)(2,1)}, bf16[3,2,80,128]{2,3,1,0:T(8,128)(2,1)}, u32[]{:S(2)}, u32[]{:S(2)}) collective-permute-start(bf16[3,2,80,128]{2,3,1,0:T(8,128)(2,1)} %get-tuple-element.1285), channel_id=1, source_target_pairs={{0,3},{1,0},{2,1},{3,2},{4,7},{5,4},{6,5},{7,6},{8,11},{9,8},{10,9... | collective-permute-start | bytes 368648 | tf_op jit(solution)/shard_map/ppermute | solution.py:18
  207.4 2.9 %copy-start.2 = (s32[1,3,3,128]{3,0,2,1:T(1,128)S(1)}, s32[1,3,3,128]{3,0,2,1:T(1,128)}, u32[]{:S(2)}) copy-start(s32[1,3,3,128]{3,0,2,1:T(1,128)} %get-tuple-element.1309) | copy-start | bytes 13828
  207.4 3.0 %copy-start.3 = (s32[1,3,3,128]{3,0,2,1:T(1,128)S(1)}, s32[1,3,3,128]{3,0,2,1:T(1,128)}, u32[]{:S(2)}) copy-start(s32[1,3,3,128]{3,0,2,1:T(1,128)} %get-tuple-element.1310) | copy-start | bytes 13828
  (9 other events, 13.2 us)
where the time goes:
time: 241 us; the launch traced here: 237 us
  matrix products  65.6 us (27%)
  starting transfers between devices  63 us (26%)
  other arithmetic  36.5 us (15%)
  waiting for transfers between devices  35.8 us (15%)
  local copies, waits for them, and re-layouts  26.8 us (11%)
  between operations  8.83 us (4%)
    dot_general x16, matrix products, one_block(): lax.dot_general(obs_gain, scaled, (((1,), (1,)), ((), ())), preferred_ele...  65.6 us
    ppermute x16, starting transfers between devices, shifted(): lax.ppermute(value, axis, [(source, source + steps) for source in range(l...  43.9 us
    ppermute x16, waiting for transfers between devices, passed_along(): return lax.ppermute(value, axis, pairs)  26 us
    ppermute x16, starting transfers between devices, passed_along(): return lax.ppermute(value, axis, pairs)  19.1 us
    while x16, local copies, waits for them, and re-layouts, assimilate(): lax.fori_loop(0, cells // block_cols, one_block, jnp.zeros_like(flat_state))  14.7 us
    ppermute x16, waiting for transfers between devices, shifted(): lax.ppermute(value, axis, [(source, source + steps) for source in range(l...  9.85 us
    reduce_sum x4, other arithmetic, assimilate(): centered = (flat_state - jnp.mean(flat_state, axis=0)).astype(jnp.bfloat16)  9.23 us
    another operation x8, other arithmetic, local(): floats_near = jnp.stack([western[0], floats_band, eastern[0]])  4.85 us
  transfers between devices with their start and end apart: 32, of which 14 were waited for; matrix products, arithmetic and copies ran while one was open for 6% of the time, Pallas kernels for 0%

commit v1 on v0

v1 whole, which is shorter than its diff:
```python
import functools

import jax
import jax.numpy as jnp
from jax import lax
from jax.experimental import pallas as pl
from jax.experimental.pallas import tpu as pltpu
from jax.sharding import PartitionSpec as P

REACH = 32
LANES = 128
GROUP = 8

OFFSETS = ((0, 0), (-1, 0), (1, 0), (-1, -1), (0, -1), (1, -1), (-1, 1), (0, 1), (1, 1))
NORTH = tuple(t for t, (dy, _) in enumerate(OFFSETS) if dy < 0)
SOUTH = tuple(t for t, (dy, _) in enumerate(OFFSETS) if dy > 0)
LEVEL = tuple(t for t, (dy, dx) in enumerate(OFFSETS) if dy == 0 and dx != 0)


def opposite(slot):
    dy, dx = OFFSETS[slot]
    return OFFSETS.index((-dy, -dx))


def split3(value):
    high = value.astype(jnp.bfloat16)
    rest = value - high.astype(jnp.float32)
    mid = rest.astype(jnp.bfloat16)
    low = rest - mid.astype(jnp.float32)
    return high.astype(jnp.float32), mid.astype(jnp.float32), low


def kernel(
    dims,
    order_s,
    count_s,
    cell_s,
    x_ref,
    value_ref,
    error_ref,
    cell_ref,
    radius_ref,
    out_ref,
    xt,
    cent,
    hx,
    packets,
    hp_all,
    gain_all,
    reach_lat,
    decay_lat,
    gap_mid,
    decay_mid,
    gap_side,
    decay_side,
    send_sem,
    recv_sem,
):
    members, rows, cols, slots, batches, n_lat, n_lon = dims
    padded = xt.shape[1]
    chunks = cols // REACH
    chunk_cells = rows * REACH
    row_groups = rows // GROUP
    block = GROUP * REACH
    f32, bf16 = jnp.float32, jnp.bfloat16
    lat = lax.axis_index("lat")
    lon = lax.axis_index("lon")
    has_north = lat > 0
    has_south = lat < n_lat - 1

    def device(slot):
        dy, dx = OFFSETS[slot]
        return (lat + dy, lax.rem(lon + dx + n_lon, n_lon))

    def at_sides(action):
        for slot in LEVEL:
            action(slot)

        @pl.when(has_north)
        def _():
            for slot in NORTH:
                action(slot)

        @pl.when(has_south)
        def _():
            for slot in SOUTH:
                action(slot)

    packets[...] = jnp.zeros_like(packets)
    barrier = pltpu.get_barrier_semaphore()

    def greet(slot):
        pl.semaphore_signal(
            barrier, inc=1, device_id=device(slot), device_id_type=pl.DeviceIdType.MESH
        )

    at_sides(greet)

    hp_all[...] = jnp.zeros_like(hp_all)
    gain_all[...] = jnp.zeros_like(gain_all)

    def centre(start, size):
        x = xt[pl.ds(start, size), :]
        mean = jnp.sum(x, axis=1, keepdims=True) * (1.0 / members)
        cent[pl.ds(start, size), :] = (x - mean).astype(bf16)

    def load_row(r, carry):
        v = x_ref[pl.ds(r, members, stride=rows), :]
        v = jnp.concatenate([v, jnp.zeros((padded - members, cols), f32)], axis=0)
        vt = jnp.transpose(v)
        mean = jnp.sum(vt, axis=1, keepdims=True) * (1.0 / members)
        vc = (vt - mean).astype(bf16)
        for q in range(chunks):
            start = pl.multiple_of(q * chunk_cells + r * REACH, REACH)
            xt[pl.ds(start, REACH), :] = vt[q * REACH : (q + 1) * REACH]
            cent[pl.ds(start, REACH), :] = vc[q * REACH : (q + 1) * REACH]
        return carry

    lax.fori_loop(0, rows, load_row, 0)

    above = (lat + n_lat - 1) // n_lat
    below = (2 * n_lat - 2 - lat) // n_lat
    pl.semaphore_wait(barrier, len(LEVEL) + len(NORTH) * above + len(SOUTH) * below)

    def outgoing(k, slot):
        there = opposite(slot)
        return pltpu.make_async_remote_copy(
            src_ref=packets.at[k, 0],
            dst_ref=packets.at[k, there],
            send_sem=send_sem.at[k, slot],
            recv_sem=recv_sem.at[k, there],
            device_id=device(slot),
            device_id_type=pl.DeviceIdType.MESH,
        )

    def incoming(k, slot):
        return pltpu.make_async_remote_copy(
            src_ref=packets.at[k, 0],
            dst_ref=packets.at[k, slot],
            send_sem=send_sem.at[k, slot],
            recv_sem=recv_sem.at[k, slot],
            device_id=device(slot),
            device_id_type=pl.DeviceIdType.MESH,
        )

    def unpack(k, slot):
        dy, dx = OFFSETS[slot]
        lanes = slice(slot * slots, (slot + 1) * slots)
        packet = packets[k, slot]
        hp = packet[:members]
        tail = packet[members:].astype(f32)
        base = tail[0:1] + tail[1:2] + tail[2:3]
        slope = tail[3:4] + tail[4:5] + tail[5:6]
        radius = tail[8:9]
        hp_all[:members, lanes] = hp
        gain_all[:members, lanes] = (base - slope * hp.astype(f32)).astype(bf16)
        reach2 = radius * radius
        rate = -2.0 / jnp.maximum(reach2, 1.0)
        row_ids = lax.broadcasted_iota(jnp.int32, (rows, slots), 0).astype(f32)
        dlat = row_ids - (tail[6:7] + float(dy * rows))
        dlat2 = dlat * dlat
        reach_lat[:, lanes] = reach2 - dlat2
        decay_lat[:, lanes] = jnp.exp(dlat2 * rate)
        if dx == 0:
            col_ids = lax.broadcasted_iota(jnp.int32, (cols, slots), 0).astype(f32)
            dlon = col_ids - tail[7:8]
            gap_ref, decay_ref, here = gap_mid, decay_mid, lanes
        else:
            first = 0 if dx < 0 else cols - REACH
            col_ids = lax.broadcasted_iota(jnp.int32, (REACH, slots), 0).astype(f32)
            dlon = col_ids + float(first - dx * cols) - tail[7:8]
            gap_ref, decay_ref = gap_side, decay_side
            here = slice((slot - 3) * slots, (slot - 2) * slots)
        dlon2 = dlon * dlon
        gap_ref[:, here] = dlon2
        decay_ref[:, here] = jnp.exp(dlon2 * rate)

    def update(q, group, first_slot, n_slots, side, centring):
        lanes = slice(first_slot * slots, (first_slot + n_slots) * slots)
        width = n_slots * slots
        cells = pl.ds(pl.multiple_of(q * chunk_cells + group * block, block), block)
        cov = jnp.dot(cent[cells, :], hp_all[:, lanes], preferred_element_type=f32)
        if side:
            here = slice((first_slot - 3) * slots, (first_slot - 3 + n_slots) * slots)
            gap, decay = gap_side[:, here], decay_side[:, here]
        else:
            columns = pl.ds(pl.multiple_of(q * REACH, REACH), REACH)
            gap, decay = gap_mid[columns, lanes], decay_mid[columns, lanes]
        lat_rows = pl.ds(pl.multiple_of(group * GROUP, GROUP), GROUP)
        reach = reach_lat[lat_rows, lanes]
        fade = decay_lat[lat_rows, lanes]
        parts = []
        for r in range(GROUP):
            weight = jnp.where(gap <= reach[r : r + 1], decay * fade[r : r + 1], 0.0)
            parts.append((cov[r * REACH : (r + 1) * REACH] * weight).astype(bf16))
        scaled = jnp.concatenate(parts, axis=0)
        inc = lax.dot_general(
            scaled, gain_all[:, lanes], (((1,), (1,)), ((), ())), preferred_element_type=f32
        )
        x = xt[cells, :] + inc
        xt[cells, :] = x
        if centring:
            mean = jnp.sum(x, axis=1, keepdims=True) * (1.0 / members)
            cent[cells, :] = (x - mean).astype(bf16)

    def sweep(first_q, n_q, first_slot, n_slots, side=False, centring=False):
        def step(i, carry):
            q = first_q + i // row_groups
            update(q, i % row_groups, first_slot, n_slots, side, centring)
            return carry

        lax.fori_loop(0, n_q * row_groups, step, 0)

    def one_batch(k, carry):
        chosen = order_s[k]

        def gather(i, inner):
            for j in range(8):
                s = i * 8 + j
                cell = cell_s[chosen, 0, 0, s]
                row = cell // cols
                col = cell % cols
                place = (col // REACH) * chunk_cells + row * REACH + col % REACH
                hx[pl.ds(s, 1), :] = xt[pl.ds(place, 1), :]
            return inner

        lax.fori_loop(0, slots // 8, gather, 0)
        prior = jnp.transpose(hx[...])[:members]
        mean = jnp.sum(prior, axis=0, keepdims=True) * (1.0 / members)
        pert = prior - mean
        var = jnp.sum(pert * pert, axis=0, keepdims=True) * (1.0 / (members - 1))
        error = error_ref[chosen, 0]
        total = var + error
        shrink = 1.0 / (1.0 + jnp.sqrt(error / total))
        factor = 1.0 / ((members - 1) * total)
        live = lax.broadcasted_iota(jnp.int32, (1, slots), 1) < count_s[chosen, 0, 0]
        base = jnp.where(live, factor * (value_ref[chosen, 0] - mean), 0.0)
        slope = jnp.where(live, factor * shrink, 0.0)
        cell = cell_ref[chosen, 0]
        tail = jnp.concatenate(
            [
                *split3(base),
                *split3(slope),
                (cell // cols).astype(f32),
                (cell % cols).astype(f32),
                radius_ref[chosen, 0].astype(f32),
                jnp.zeros((7, slots), f32),
            ],
            axis=0,
        )
        packets[k, 0, :members, :] = jnp.where(live, pert, 0.0).astype(bf16)
        packets[k, 0, members:, :] = tail.astype(bf16)
        at_sides(lambda slot: outgoing(k, slot).start())

        unpack(k, 0)
        sweep(0, chunks, 0, 1)

        @pl.when(has_north)
        def _():
            incoming(k, 1).wait_recv()

        @pl.when(has_south)
        def _():
            incoming(k, 2).wait_recv()

        unpack(k, 1)
        unpack(k, 2)
        sweep(1, chunks - 2, 1, 2, centring=True)
        sweep(0, 1, 1, 2)
        sweep(chunks - 1, 1, 1, 2)

        for slot in LEVEL:
            incoming(k, slot).wait_recv()

        @pl.when(has_north)
        def _():
            for slot in NORTH[1:]:
                incoming(k, slot).wait_recv()

        @pl.when(has_south)
        def _():
            for slot in SOUTH[1:]:
                incoming(k, slot).wait_recv()

        for slot in range(3, 9):
            unpack(k, slot)
        sweep(0, 1, 3, 3, side=True, centring=True)
        sweep(chunks - 1, 1, 6, 3, side=True, centring=True)
        at_sides(lambda slot: outgoing(k, slot).wait_send())
        return carry

    lax.fori_loop(0, batches, one_batch, 0)

    def store_row(r, carry):
        pieces = [
            xt[pl.ds(pl.multiple_of(q * chunk_cells + r * REACH, REACH), REACH), :]
            for q in range(chunks)
        ]
        v = jnp.transpose(jnp.concatenate(pieces, axis=0))
        out_ref[pl.ds(r, members, stride=rows), :] = v[:members]
        return carry

    lax.fori_loop(0, rows, store_row, 0)


def local(ensemble, obs_value, obs_error, obs_cell, obs_radius, obs_count, batch_order):
    members, levels, rows, cols = ensemble.shape
    batches = obs_cell.shape[0]
    slots = obs_cell.shape[-1]
    assert levels == 1 and cols == LANES and slots == LANES and rows == REACH
    n_lat, n_lon = lax.axis_size("lat"), lax.axis_size("lon")
    padded = -(-members // LANES) * LANES
    cells = rows * cols
    tiles = len(OFFSETS)
    vmem = pl.BlockSpec(memory_space=pltpu.VMEM)
    smem = pl.BlockSpec(memory_space=pltpu.SMEM)
    f32, bf16 = jnp.float32, jnp.bfloat16
    out = pl.pallas_call(
        functools.partial(kernel, (members, rows, cols, slots, batches, n_lat, n_lon)),
        out_shape=jax.ShapeDtypeStruct((members * rows, cols), f32),
        in_specs=[smem, smem, smem, vmem, vmem, vmem, vmem, vmem],
        out_specs=vmem,
        scratch_shapes=[
            pltpu.VMEM((cells, padded), f32),
            pltpu.VMEM((cells, padded), bf16),
            pltpu.VMEM((slots, padded), f32),
            pltpu.VMEM((batches, tiles, members + 16, slots), bf16),
            pltpu.VMEM((padded, tiles * slots), bf16),
            pltpu.VMEM((padded, tiles * slots), bf16),
            pltpu.VMEM((rows, tiles * slots), f32),
            pltpu.VMEM((rows, tiles * slots), f32),
            pltpu.VMEM((cols, 3 * slots), f32),
            pltpu.VMEM((cols, 3 * slots), f32),
            pltpu.VMEM((REACH, 6 * slots), f32),
            pltpu.VMEM((REACH, 6 * slots), f32),
            pltpu.SemaphoreType.DMA((batches, tiles)),
            pltpu.SemaphoreType.DMA((batches, tiles)),
        ],
        compiler_params=pltpu.CompilerParams(
            collective_id=0, has_side_effects=True, vmem_limit_bytes=32 * 1024 * 1024
        ),
    )(
        batch_order,
        obs_count,
        obs_cell,
        ensemble.reshape(members * rows, cols),
        obs_value,
        obs_error,
        obs_cell,
        obs_radius,
    )
    return out.reshape(ensemble.shape)


def solution(mesh):
    return jax.shard_map(
        local,
        mesh=mesh,
        in_specs=(
            P(None, None, "lat", "lon"),
            P(None, "lat", "lon", None),
            P(None, "lat", "lon", None),
            P(None, "lat", "lon", None),
            P(None, "lat", "lon", None),
            P(None, "lat", "lon"),
            P(),
        ),
        out_specs=P(None, None, "lat", "lon"),
        check_vma=False,
    )
```

time: 241 us -> 82 us (0.34); the launches traced: 237 us -> 81.8 us
  Pallas kernels: 0 us -> 75.3 us
  matrix products: 65.6 us -> 0 us
  starting transfers between devices: 63 us -> 0 us
  other arithmetic: 36.5 us -> 0 us
  waiting for transfers between devices: 35.8 us -> 0 us
  local copies, waits for them, and re-layouts: 26.8 us -> 6.49 us
  between operations: 8.83 us -> 0.02 us
    pallas_call x0 -> x1, Pallas kernels: none -> 75.3 us  [local(): pl.pallas_call(functools.partial(kernel, (members, rows, cols, slots, bat...]
    dot_general x16 -> x0, matrix products: 65.6 us -> none  [one_block(): lax.dot_general(obs_gain, scaled, (((1,), (1,)), ((), ())), preferred_ele...]
    ppermute x32 -> x0, starting transfers between devices: 63 us -> none  [the longest x16 43.9 us: shifted(): lax.ppermute(value, axis, [(source, source + steps) for source in range(l...]
    ppermute x32 -> x0, waiting for transfers between devices: 35.8 us -> none  [the longest x16 26 us: passed_along(): return lax.ppermute(value, axis, pairs)]
    while x16 -> x0, local copies, waits for them, and re-layouts: 14.7 us -> none  [assimilate(): lax.fori_loop(0, cells // block_cols, one_block, jnp.zeros_like(flat_state))]
    reduce_sum x12 -> x0, other arithmetic: 10.6 us -> none  [the longest x4 9.23 us: assimilate(): centered = (flat_state - jnp.mean(flat_state, axis=0)).astype(jnp.bfloat16)]
    another operation x56 -> x0, other arithmetic: 7.02 us -> none  [the longest x8 4.85 us: local(): floats_near = jnp.stack([western[0], floats_band, eastern[0]])]
    convert_element_type x8 -> x0, other arithmetic: 5.97 us -> none  [the longest x4 4.16 us: assimilate(): centered = (flat_state - jnp.mean(flat_state, axis=0)).astype(jnp.bfloat16)]
  transfers between devices with their start and end apart: 32 -> 0, of which waited for: 14 -> 0; matrix products, arithmetic and copies ran while one was open for 6% -> 0% of each run, Pallas kernels for 0% -> 0%
where the time goes in v1:
time: 82 us; the launch traced here: 81.8 us
  Pallas kernels  75.3 us (92%)
  local copies, waits for them, and re-layouts  6.49 us (8%)
    pallas_call x1, Pallas kernels, local(): pl.pallas_call(functools.partial(kernel, (members, rows, cols, slots, bat...  75.3 us
    unnamed x14, local copies, waits for them, and re-layouts  6.49 us

profile of v1, /device:TPU:17, one launch (start us, length us, event | category | flops | bytes accessed | tf_op | source)
XLA Modules:
  0.0 81.8 jit_solution(1965381131328249968)
XLA Ops:
  0.0 0.7 copy.8.count_s
  0.7 0.0 copy-start
  0.7 1.3 %copy-done = f32[80,1,32,128]{3,2,1,0:T(8,128)S(1)} copy-done((f32[80,1,32,128]{3,2,1,0:T(8,128)S(1)}, f32[80,1,32,128]{3,2,1,0:T(8,128)}, u32[]{:S(2)}) %copy-start) | copy-done | bytes 1310744
  2.1 0.0 copy-start.1
  2.1 0.7 copy-done.1
  2.7 0.0 copy-start.2
  2.7 0.7 copy-done.2
  3.4 0.0 copy-start.3
  3.4 0.7 copy-done.3
  4.1 0.0 copy-start.4
  4.1 0.7 copy-done.4
  4.8 0.0 copy-start.5
  4.8 0.7 copy-done.5
  5.4 75.3 %shard_map.73 = f32[2560,128]{1,0:T(8,128)S(1)} custom-call(s32[4]{0:T(128)S(1)} %copy-done.5, s32[4,1,1]{2,1,0:T(1,128)S(1)} %copy.8.count_s, s32[4,1,1,128]{3,2,1,0:T(1,128)S(1)} %copy-done.1, f32[2560,128]{1,0:T(8,128)S(1)} %bitcast.5, f32[4,1,1,128]{3,2,1,0:T(1,128)S(1)} %copy-done.2, f32[4,1,1,128]{3,2,1,0:T(1,128)S(1)} %copy-done.3, ...), custom_call_target="tpu_custom_call" | custom-call | tf_op jit(solution)/shard_map/pallas_call | solution.py:318
  80.7 1.1 %copy.11 = f32[80,1,32,128]{3,2,1,0:T(8,128)} copy(f32[80,1,32,128]{3,2,1,0:T(8,128)S(1)} %bitcast.4) | data formatting | bytes 2621440
Async XLA Ops:
  0.7 1.3 %copy-start = (f32[80,1,32,128]{3,2,1,0:T(8,128)S(1)}, f32[80,1,32,128]{3,2,1,0:T(8,128)}, u32[]{:S(2)}) copy-start(f32[80,1,32,128]{3,2,1,0:T(8,128)} %param.7) | copy-start | bytes 3932164
  2.1 0.7 copy-start.1
  2.7 0.7 copy-start.2
  3.4 0.7 copy-start.3
  4.1 0.7 copy-start.4
  4.8 0.7 copy-start.5

commit v2 on v1

--- a/solution.py
+++ b/solution.py
@@ -9,25 +9,28 @@
 
 REACH = 32
 LANES = 128
+COL_BITS = 7
+REACH_BITS = 5
+TAIL = 16
+UNROLL = 8
 GROUP = 8
 
 OFFSETS = ((0, 0), (-1, 0), (1, 0), (-1, -1), (0, -1), (1, -1), (-1, 1), (0, 1), (1, 1))
-NORTH = tuple(t for t, (dy, _) in enumerate(OFFSETS) if dy < 0)
-SOUTH = tuple(t for t, (dy, _) in enumerate(OFFSETS) if dy > 0)
-LEVEL = tuple(t for t, (dy, dx) in enumerate(OFFSETS) if dy == 0 and dx != 0)
+NORTH, SOUTH, WEST, EAST = 1, 2, 4, 7
+
+
+def repeat(count, unroll, body):
+    def step(i, carry):
+        for j in range(unroll):
+            body(i * unroll + j)
+        return carry
+
+    lax.fori_loop(0, count // unroll, step, 0)
 
 
 def opposite(slot):
     dy, dx = OFFSETS[slot]
     return OFFSETS.index((-dy, -dx))
-
-
-def split3(value):
-    high = value.astype(jnp.bfloat16)
-    rest = value - high.astype(jnp.float32)
-    mid = rest.astype(jnp.bfloat16)
-    low = rest - mid.astype(jnp.float32)
-    return high.astype(jnp.float32), mid.astype(jnp.float32), low
 
 
 def kernel(
@@ -73,17 +76,17 @@
         return (lat + dy, lax.rem(lon + dx + n_lon, n_lon))
 
     def at_sides(action):
-        for slot in LEVEL:
+        for slot in (WEST, EAST):
             action(slot)
 
         @pl.when(has_north)
         def _():
-            for slot in NORTH:
+            for slot in (1, 3, 6):
                 action(slot)
 
         @pl.when(has_south)
         def _():
-            for slot in SOUTH:
+            for slot in (2, 5, 8):
                 action(slot)
 
     packets[...] = jnp.zeros_like(packets)
@@ -104,7 +107,7 @@
         mean = jnp.sum(x, axis=1, keepdims=True) * (1.0 / members)
         cent[pl.ds(start, size), :] = (x - mean).astype(bf16)
 
-    def load_row(r, carry):
+    def load_row(r):
         v = x_ref[pl.ds(r, members, stride=rows), :]
         v = jnp.concatenate([v, jnp.zeros((padded - members, cols), f32)], axis=0)
         vt = jnp.transpose(v)
@@ -114,61 +117,53 @@
             start = pl.multiple_of(q * chunk_cells + r * REACH, REACH)
             xt[pl.ds(start, REACH), :] = vt[q * REACH : (q + 1) * REACH]
             cent[pl.ds(start, REACH), :] = vc[q * REACH : (q + 1) * REACH]
-        return carry
-
-    lax.fori_loop(0, rows, load_row, 0)
+
+    repeat(rows, 4, load_row)
 
     above = (lat + n_lat - 1) // n_lat
     below = (2 * n_lat - 2 - lat) // n_lat
-    pl.semaphore_wait(barrier, len(LEVEL) + len(NORTH) * above + len(SOUTH) * below)
-
-    def outgoing(k, slot):
-        there = opposite(slot)
+    pl.semaphore_wait(barrier, 2 + 3 * above + 3 * below)
+
+    def moved(k, source, target, sender, toward):
         return pltpu.make_async_remote_copy(
-            src_ref=packets.at[k, 0],
-            dst_ref=packets.at[k, there],
-            send_sem=send_sem.at[k, slot],
-            recv_sem=recv_sem.at[k, there],
-            device_id=device(slot),
+            src_ref=packets.at[k, source],
+            dst_ref=packets.at[k, target],
+            send_sem=send_sem.at[k, sender],
+            recv_sem=recv_sem.at[k, target],
+            device_id=device(toward),
             device_id_type=pl.DeviceIdType.MESH,
         )
 
+    def outgoing(k, slot):
+        return moved(k, 0, opposite(slot), slot, slot)
+
     def incoming(k, slot):
-        return pltpu.make_async_remote_copy(
-            src_ref=packets.at[k, 0],
-            dst_ref=packets.at[k, slot],
-            send_sem=send_sem.at[k, slot],
-            recv_sem=recv_sem.at[k, slot],
-            device_id=device(slot),
-            device_id_type=pl.DeviceIdType.MESH,
-        )
+        return moved(k, 0, slot, slot, EAST)
 
     def unpack(k, slot):
         dy, dx = OFFSETS[slot]
         lanes = slice(slot * slots, (slot + 1) * slots)
         packet = packets[k, slot]
         hp = packet[:members]
-        tail = packet[members:].astype(f32)
-        base = tail[0:1] + tail[1:2] + tail[2:3]
-        slope = tail[3:4] + tail[4:5] + tail[5:6]
-        radius = tail[8:9]
+        tail = packet[2 * members :].astype(f32)
+        radius = tail[2:3]
         hp_all[:members, lanes] = hp
-        gain_all[:members, lanes] = (base - slope * hp.astype(f32)).astype(bf16)
+        gain_all[:members, lanes] = packet[members : 2 * members]
         reach2 = radius * radius
         rate = -2.0 / jnp.maximum(reach2, 1.0)
         row_ids = lax.broadcasted_iota(jnp.int32, (rows, slots), 0).astype(f32)
-        dlat = row_ids - (tail[6:7] + float(dy * rows))
+        dlat = row_ids - (tail[0:1] + float(dy * rows))
         dlat2 = dlat * dlat
         reach_lat[:, lanes] = reach2 - dlat2
         decay_lat[:, lanes] = jnp.exp(dlat2 * rate)
         if dx == 0:
             col_ids = lax.broadcasted_iota(jnp.int32, (cols, slots), 0).astype(f32)
-            dlon = col_ids - tail[7:8]
+            dlon = col_ids - tail[1:2]
             gap_ref, decay_ref, here = gap_mid, decay_mid, lanes
         else:
             first = 0 if dx < 0 else cols - REACH
             col_ids = lax.broadcasted_iota(jnp.int32, (REACH, slots), 0).astype(f32)
-            dlon = col_ids + float(first - dx * cols) - tail[7:8]
+            dlon = col_ids + float(first - dx * cols) - tail[1:2]
             gap_ref, decay_ref = gap_side, decay_side
             here = slice((slot - 3) * slots, (slot - 2) * slots)
         dlon2 = dlon * dlon
@@ -204,27 +199,26 @@
             cent[cells, :] = (x - mean).astype(bf16)
 
     def sweep(first_q, n_q, first_slot, n_slots, side=False, centring=False):
-        def step(i, carry):
+        def step(i):
             q = first_q + i // row_groups
             update(q, i % row_groups, first_slot, n_slots, side, centring)
-            return carry
-
-        lax.fori_loop(0, n_q * row_groups, step, 0)
+
+        repeat(n_q * row_groups, min(UNROLL, n_q * row_groups), step)
 
     def one_batch(k, carry):
         chosen = order_s[k]
 
         def gather(i, inner):
-            for j in range(8):
-                s = i * 8 + j
+            for j in range(16):
+                s = i * 16 + j
                 cell = cell_s[chosen, 0, 0, s]
-                row = cell // cols
-                col = cell % cols
-                place = (col // REACH) * chunk_cells + row * REACH + col % REACH
+                chunk = (cell & (cols - 1)) >> REACH_BITS
+                row = cell >> COL_BITS
+                place = chunk * chunk_cells + row * REACH + (cell & (REACH - 1))
                 hx[pl.ds(s, 1), :] = xt[pl.ds(place, 1), :]
             return inner
 
-        lax.fori_loop(0, slots // 8, gather, 0)
+        lax.fori_loop(0, slots // 16, gather, 0)
         prior = jnp.transpose(hx[...])[:members]
         mean = jnp.sum(prior, axis=0, keepdims=True) * (1.0 / members)
         pert = prior - mean
@@ -234,54 +228,52 @@
         shrink = 1.0 / (1.0 + jnp.sqrt(error / total))
         factor = 1.0 / ((members - 1) * total)
         live = lax.broadcasted_iota(jnp.int32, (1, slots), 1) < count_s[chosen, 0, 0]
-        base = jnp.where(live, factor * (value_ref[chosen, 0] - mean), 0.0)
-        slope = jnp.where(live, factor * shrink, 0.0)
+        gain = factor * (value_ref[chosen, 0] - mean - shrink * pert)
         cell = cell_ref[chosen, 0]
         tail = jnp.concatenate(
             [
-                *split3(base),
-                *split3(slope),
-                (cell // cols).astype(f32),
-                (cell % cols).astype(f32),
+                (cell >> COL_BITS).astype(f32),
+                (cell & (cols - 1)).astype(f32),
                 radius_ref[chosen, 0].astype(f32),
-                jnp.zeros((7, slots), f32),
+                jnp.zeros((TAIL - 3, slots), f32),
             ],
             axis=0,
         )
         packets[k, 0, :members, :] = jnp.where(live, pert, 0.0).astype(bf16)
-        packets[k, 0, members:, :] = tail.astype(bf16)
+        packets[k, 0, members : 2 * members, :] = jnp.where(live, gain, 0.0).astype(bf16)
+        packets[k, 0, 2 * members :, :] = tail.astype(bf16)
         at_sides(lambda slot: outgoing(k, slot).start())
 
         unpack(k, 0)
         sweep(0, chunks, 0, 1)
 
+
         @pl.when(has_north)
         def _():
-            incoming(k, 1).wait_recv()
+            incoming(k, NORTH).wait_recv()
 
         @pl.when(has_south)
         def _():
-            incoming(k, 2).wait_recv()
-
-        unpack(k, 1)
-        unpack(k, 2)
+            incoming(k, SOUTH).wait_recv()
+
+        for slot in (NORTH, SOUTH):
+            unpack(k, slot)
         sweep(1, chunks - 2, 1, 2, centring=True)
         sweep(0, 1, 1, 2)
         sweep(chunks - 1, 1, 1, 2)
 
-        for slot in LEVEL:
+        @pl.when(has_north)
+        def _():
+            for slot in (3, 6):
+                incoming(k, slot).wait_recv()
+
+        @pl.when(has_south)
+        def _():
+            for slot in (5, 8):
+                incoming(k, slot).wait_recv()
+
+        for slot in (WEST, EAST):
             incoming(k, slot).wait_recv()
-
-        @pl.when(has_north)
-        def _():
-            for slot in NORTH[1:]:
-                incoming(k, slot).wait_recv()
-
-        @pl.when(has_south)
-        def _():
-            for slot in SOUTH[1:]:
-                incoming(k, slot).wait_recv()
-
         for slot in range(3, 9):
             unpack(k, slot)
         sweep(0, 1, 3, 3, side=True, centring=True)
@@ -291,16 +283,15 @@
 
     lax.fori_loop(0, batches, one_batch, 0)
 
-    def store_row(r, carry):
+    def store_row(r):
         pieces = [
             xt[pl.ds(pl.multiple_of(q * chunk_cells + r * REACH, REACH), REACH), :]
             for q in range(chunks)
         ]
         v = jnp.transpose(jnp.concatenate(pieces, axis=0))
         out_ref[pl.ds(r, members, stride=rows), :] = v[:members]
-        return carry
-
-    lax.fori_loop(0, rows, store_row, 0)
+
+    repeat(rows, 4, store_row)
 
 
 def local(ensemble, obs_value, obs_error, obs_cell, obs_radius, obs_count, batch_order):
@@ -324,7 +315,7 @@
             pltpu.VMEM((cells, padded), f32),
             pltpu.VMEM((cells, padded), bf16),
             pltpu.VMEM((slots, padded), f32),
-            pltpu.VMEM((batches, tiles, members + 16, slots), bf16),
+            pltpu.VMEM((batches, tiles, 2 * members + TAIL, slots), bf16),
             pltpu.VMEM((padded, tiles * slots), bf16),
             pltpu.VMEM((padded, tiles * slots), bf16),
             pltpu.VMEM((rows, tiles * slots), f32),

time: 82 us -> 52.4 us (0.64)
  Pallas kernels: 75.3 us -> 45.6 us
    pallas_call x1, Pallas kernels: 75.3 us -> 45.6 us  [local(): pl.pallas_call(functools.partial(kernel, (members, rows, cols, slots, bat...]
where the time goes in v2:
time: 52.4 us; the launch traced here: 52.1 us
  Pallas kernels  45.6 us (87%)
  local copies, waits for them, and re-layouts  6.49 us (12%)
    pallas_call x1, Pallas kernels, local(): pl.pallas_call(functools.partial(kernel, (members, rows, cols, slots, bat...  45.6 us
    unnamed x14, local copies, waits for them, and re-layouts  6.49 us

profile of v2, /device:TPU:17, one launch (start us, length us, event | category | flops | bytes accessed | tf_op | source)
XLA Modules:
  0.0 52.1 jit_solution(15231958551033396928)
XLA Ops:
  0.0 0.7 %copy.8.count_s = s32[4,1,1]{2,1,0:T(1,128)S(1)} copy(s32[4,1,1]{0,2,1:T(1,128)} %param.12) | data formatting | bytes 32 | tf_op args[5]
  0.7 0.0 copy-start
  0.7 1.3 %copy-done = f32[80,1,32,128]{3,2,1,0:T(8,128)S(1)} copy-done((f32[80,1,32,128]{3,2,1,0:T(8,128)S(1)}, f32[80,1,32,128]{3,2,1,0:T(8,128)}, u32[]{:S(2)}) %copy-start) | copy-done | bytes 1310744
  2.1 0.0 copy-start.1
  2.1 0.7 %copy-done.1 = s32[4,1,1,128]{3,2,1,0:T(1,128)S(1)} copy-done((s32[4,1,1,128]{3,2,1,0:T(1,128)S(1)}, s32[4,1,1,128]{3,2,1,0:T(1,128)}, u32[]{:S(2)}) %copy-start.1) | copy-done | bytes 2072
  2.7 0.0 copy-start.2
  2.7 0.7 %copy-done.2 = f32[4,1,1,128]{3,2,1,0:T(1,128)S(1)} copy-done((f32[4,1,1,128]{3,2,1,0:T(1,128)S(1)}, f32[4,1,1,128]{3,2,1,0:T(1,128)}, u32[]{:S(2)}) %copy-start.2) | copy-done | bytes 2072
  3.4 0.0 copy-start.3
  3.4 0.7 %copy-done.3 = f32[4,1,1,128]{3,2,1,0:T(1,128)S(1)} copy-done((f32[4,1,1,128]{3,2,1,0:T(1,128)S(1)}, f32[4,1,1,128]{3,2,1,0:T(1,128)}, u32[]{:S(2)}) %copy-start.3) | copy-done | bytes 2072
  4.1 0.0 copy-start.4
  4.1 0.7 %copy-done.4 = s32[4,1,1,128]{3,2,1,0:T(1,128)S(1)} copy-done((s32[4,1,1,128]{3,2,1,0:T(1,128)S(1)}, s32[4,1,1,128]{3,2,1,0:T(1,128)}, u32[]{:S(2)}) %copy-start.4) | copy-done | bytes 2072
  4.8 0.0 copy-start.5
  4.8 0.7 %copy-done.5 = s32[4]{0:T(128)S(1)} copy-done((s32[4]{0:T(128)S(1)}, s32[4]{0:T(128)}, u32[]{:S(2)}) %copy-start.5) | copy-done | bytes 40
  5.4 45.6 %shard_map.73 = f32[2560,128]{1,0:T(8,128)S(1)} custom-call(s32[4]{0:T(128)S(1)} %copy-done.5, s32[4,1,1]{2,1,0:T(1,128)S(1)} %copy.8.count_s, s32[4,1,1,128]{3,2,1,0:T(1,128)S(1)} %copy-done.1, f32[2560,128]{1,0:T(8,128)S(1)} %bitcast.5, f32[4,1,1,128]{3,2,1,0:T(1,128)S(1)} %copy-done.2, f32[4,1,1,128]{3,2,1,0:T(1,128)S(1)} %copy-done.3, ...), custom_call_target="tpu_custom_call" | custom-call | tf_op jit(solution)/shard_map/pallas_call | solution.py:309
  51.0 1.1 %copy.11 = f32[80,1,32,128]{3,2,1,0:T(8,128)} copy(f32[80,1,32,128]{3,2,1,0:T(8,128)S(1)} %bitcast.4) | data formatting | bytes 2621440
Async XLA Ops:
  0.7 1.3 %copy-start = (f32[80,1,32,128]{3,2,1,0:T(8,128)S(1)}, f32[80,1,32,128]{3,2,1,0:T(8,128)}, u32[]{:S(2)}) copy-start(f32[80,1,32,128]{3,2,1,0:T(8,128)} %param.7) | copy-start | bytes 3932164
  2.1 0.7 %copy-start.1 = (s32[4,1,1,128]{3,2,1,0:T(1,128)S(1)}, s32[4,1,1,128]{3,2,1,0:T(1,128)}, u32[]{:S(2)}) copy-start(s32[4,1,1,128]{3,2,1,0:T(1,128)} %cell_ref.1) | copy-start | bytes 6148
  2.7 0.7 %copy-start.2 = (f32[4,1,1,128]{3,2,1,0:T(1,128)S(1)}, f32[4,1,1,128]{3,2,1,0:T(1,128)}, u32[]{:S(2)}) copy-start(f32[4,1,1,128]{3,2,1,0:T(1,128)} %value_ref.1) | copy-start | bytes 6148
  3.4 0.7 %copy-start.3 = (f32[4,1,1,128]{3,2,1,0:T(1,128)S(1)}, f32[4,1,1,128]{3,2,1,0:T(1,128)}, u32[]{:S(2)}) copy-start(f32[4,1,1,128]{3,2,1,0:T(1,128)} %error_ref.1) | copy-start | bytes 6148
  4.1 0.7 %copy-start.4 = (s32[4,1,1,128]{3,2,1,0:T(1,128)S(1)}, s32[4,1,1,128]{3,2,1,0:T(1,128)}, u32[]{:S(2)}) copy-start(s32[4,1,1,128]{3,2,1,0:T(1,128)} %radius_ref.1) | copy-start | bytes 6148
  4.8 0.7 %copy-start.5 = (s32[4]{0:T(128)S(1)}, s32[4]{0:T(128)}, u32[]{:S(2)}) copy-start(s32[4]{0:T(128)} %order_s.1) | copy-start | bytes 52

commit v3 on v2

--- a/solution.py
+++ b/solution.py
@@ -17,6 +17,8 @@
 
 OFFSETS = ((0, 0), (-1, 0), (1, 0), (-1, -1), (0, -1), (1, -1), (-1, 1), (0, 1), (1, 1))
 NORTH, SOUTH, WEST, EAST = 1, 2, 4, 7
+PASSED_NORTH = ((WEST, 5), (EAST, 8))
+PASSED_SOUTH = ((WEST, 3), (EAST, 6))
 
 
 def repeat(count, unroll, body):
@@ -81,13 +83,11 @@
 
         @pl.when(has_north)
         def _():
-            for slot in (1, 3, 6):
-                action(slot)
+            action(NORTH)
 
         @pl.when(has_south)
         def _():
-            for slot in (2, 5, 8):
-                action(slot)
+            action(SOUTH)
 
     packets[...] = jnp.zeros_like(packets)
     barrier = pltpu.get_barrier_semaphore()
@@ -122,7 +122,7 @@
 
     above = (lat + n_lat - 1) // n_lat
     below = (2 * n_lat - 2 - lat) // n_lat
-    pl.semaphore_wait(barrier, 2 + 3 * above + 3 * below)
+    pl.semaphore_wait(barrier, 2 + above + below)
 
     def moved(k, source, target, sender, toward):
         return pltpu.make_async_remote_copy(
@@ -139,6 +139,17 @@
 
     def incoming(k, slot):
         return moved(k, 0, slot, slot, EAST)
+
+    def pass_on(k, action):
+        for passed, toward, present in (
+            (PASSED_NORTH, NORTH, has_north),
+            (PASSED_SOUTH, SOUTH, has_south),
+        ):
+
+            @pl.when(present)
+            def _():
+                for source, target in passed:
+                    action(moved(k, source, target, target, toward))
 
     def unpack(k, slot):
         dy, dx = OFFSETS[slot]
@@ -247,6 +258,9 @@
         unpack(k, 0)
         sweep(0, chunks, 0, 1)
 
+        for slot in (WEST, EAST):
+            incoming(k, slot).wait_recv()
+        pass_on(k, lambda copy: copy.start())
 
         @pl.when(has_north)
         def _():
@@ -256,7 +270,7 @@
         def _():
             incoming(k, SOUTH).wait_recv()
 
-        for slot in (NORTH, SOUTH):
+        for slot in (NORTH, SOUTH, WEST, EAST):
             unpack(k, slot)
         sweep(1, chunks - 2, 1, 2, centring=True)
         sweep(0, 1, 1, 2)
@@ -264,21 +278,20 @@
 
         @pl.when(has_north)
         def _():
-            for slot in (3, 6):
+            for _, slot in PASSED_SOUTH:
                 incoming(k, slot).wait_recv()
 
         @pl.when(has_south)
         def _():
-            for slot in (5, 8):
+            for _, slot in PASSED_NORTH:
                 incoming(k, slot).wait_recv()
 
-        for slot in (WEST, EAST):
-            incoming(k, slot).wait_recv()
-        for slot in range(3, 9):
+        for _, slot in PASSED_NORTH + PASSED_SOUTH:
             unpack(k, slot)
         sweep(0, 1, 3, 3, side=True, centring=True)
         sweep(chunks - 1, 1, 6, 3, side=True, centring=True)
         at_sides(lambda slot: outgoing(k, slot).wait_send())
+        pass_on(k, lambda copy: copy.wait_send())
         return carry
 
     lax.fori_loop(0, batches, one_batch, 0)

time: 52.4 us -> 49.4 us (0.943)
  Pallas kernels: 45.6 us -> 42.4 us
    pallas_call x1, Pallas kernels: 45.6 us -> 42.4 us  [local(): pl.pallas_call(functools.partial(kernel, (members, rows, cols, slots, bat...]
where the time goes in v3:
time: 49.4 us; the launch traced here: 48.9 us
  Pallas kernels  42.4 us (86%)
  local copies, waits for them, and re-layouts  6.49 us (13%)
    pallas_call x1, Pallas kernels, local(): pl.pallas_call(functools.partial(kernel, (members, rows, cols, slots, bat...  42.4 us
    unnamed x14, local copies, waits for them, and re-layouts  6.49 us

profile of v3, /device:TPU:17, one launch (start us, length us, event | category | flops | bytes accessed | tf_op | source)
XLA Modules:
  0.0 48.9 jit_solution(16237084610650290462)
XLA Ops:
  0.0 0.7 %copy.8.count_s = s32[4,1,1]{2,1,0:T(1,128)S(1)} copy(s32[4,1,1]{0,2,1:T(1,128)} %param.12) | data formatting | bytes 32 | tf_op args[5]
  0.7 0.0 copy-start
  0.7 1.3 %copy-done = f32[80,1,32,128]{3,2,1,0:T(8,128)S(1)} copy-done((f32[80,1,32,128]{3,2,1,0:T(8,128)S(1)}, f32[80,1,32,128]{3,2,1,0:T(8,128)}, u32[]{:S(2)}) %copy-start) | copy-done | bytes 1310744
  2.1 0.0 copy-start.1
  2.1 0.7 %copy-done.1 = s32[4,1,1,128]{3,2,1,0:T(1,128)S(1)} copy-done((s32[4,1,1,128]{3,2,1,0:T(1,128)S(1)}, s32[4,1,1,128]{3,2,1,0:T(1,128)}, u32[]{:S(2)}) %copy-start.1) | copy-done | bytes 2072
  2.7 0.0 copy-start.2
  2.7 0.7 %copy-done.2 = f32[4,1,1,128]{3,2,1,0:T(1,128)S(1)} copy-done((f32[4,1,1,128]{3,2,1,0:T(1,128)S(1)}, f32[4,1,1,128]{3,2,1,0:T(1,128)}, u32[]{:S(2)}) %copy-start.2) | copy-done | bytes 2072
  3.4 0.0 copy-start.3
  3.4 0.7 %copy-done.3 = f32[4,1,1,128]{3,2,1,0:T(1,128)S(1)} copy-done((f32[4,1,1,128]{3,2,1,0:T(1,128)S(1)}, f32[4,1,1,128]{3,2,1,0:T(1,128)}, u32[]{:S(2)}) %copy-start.3) | copy-done | bytes 2072
  4.1 0.0 copy-start.4
  4.1 0.7 %copy-done.4 = s32[4,1,1,128]{3,2,1,0:T(1,128)S(1)} copy-done((s32[4,1,1,128]{3,2,1,0:T(1,128)S(1)}, s32[4,1,1,128]{3,2,1,0:T(1,128)}, u32[]{:S(2)}) %copy-start.4) | copy-done | bytes 2072
  4.8 0.0 copy-start.5
  4.8 0.7 %copy-done.5 = s32[4]{0:T(128)S(1)} copy-done((s32[4]{0:T(128)S(1)}, s32[4]{0:T(128)}, u32[]{:S(2)}) %copy-start.5) | copy-done | bytes 40
  5.4 42.4 %shard_map.73 = f32[2560,128]{1,0:T(8,128)S(1)} custom-call(s32[4]{0:T(128)S(1)} %copy-done.5, s32[4,1,1]{2,1,0:T(1,128)S(1)} %copy.8.count_s, s32[4,1,1,128]{3,2,1,0:T(1,128)S(1)} %copy-done.1, f32[2560,128]{1,0:T(8,128)S(1)} %bitcast.5, f32[4,1,1,128]{3,2,1,0:T(1,128)S(1)} %copy-done.2, f32[4,1,1,128]{3,2,1,0:T(1,128)S(1)} %copy-done.3, ...), custom_call_target="tpu_custom_call" | custom-call | tf_op jit(solution)/shard_map/pallas_call | solution.py:322
  47.8 1.1 %copy.11 = f32[80,1,32,128]{3,2,1,0:T(8,128)} copy(f32[80,1,32,128]{3,2,1,0:T(8,128)S(1)} %bitcast.4) | data formatting | bytes 2621440
Async XLA Ops:
  0.7 1.3 %copy-start = (f32[80,1,32,128]{3,2,1,0:T(8,128)S(1)}, f32[80,1,32,128]{3,2,1,0:T(8,128)}, u32[]{:S(2)}) copy-start(f32[80,1,32,128]{3,2,1,0:T(8,128)} %param.7) | copy-start | bytes 3932164
  2.1 0.7 %copy-start.1 = (s32[4,1,1,128]{3,2,1,0:T(1,128)S(1)}, s32[4,1,1,128]{3,2,1,0:T(1,128)}, u32[]{:S(2)}) copy-start(s32[4,1,1,128]{3,2,1,0:T(1,128)} %cell_ref.1) | copy-start | bytes 6148
  2.7 0.7 %copy-start.2 = (f32[4,1,1,128]{3,2,1,0:T(1,128)S(1)}, f32[4,1,1,128]{3,2,1,0:T(1,128)}, u32[]{:S(2)}) copy-start(f32[4,1,1,128]{3,2,1,0:T(1,128)} %value_ref.1) | copy-start | bytes 6148
  3.4 0.7 %copy-start.3 = (f32[4,1,1,128]{3,2,1,0:T(1,128)S(1)}, f32[4,1,1,128]{3,2,1,0:T(1,128)}, u32[]{:S(2)}) copy-start(f32[4,1,1,128]{3,2,1,0:T(1,128)} %error_ref.1) | copy-start | bytes 6148
  4.1 0.7 %copy-start.4 = (s32[4,1,1,128]{3,2,1,0:T(1,128)S(1)}, s32[4,1,1,128]{3,2,1,0:T(1,128)}, u32[]{:S(2)}) copy-start(s32[4,1,1,128]{3,2,1,0:T(1,128)} %radius_ref.1) | copy-start | bytes 6148
  4.8 0.7 %copy-start.5 = (s32[4]{0:T(128)S(1)}, s32[4]{0:T(128)}, u32[]{:S(2)}) copy-start(s32[4]{0:T(128)} %order_s.1) | copy-start | bytes 52

commit v4 on v3

--- a/solution.py
+++ b/solution.py
@@ -118,7 +118,7 @@
             xt[pl.ds(start, REACH), :] = vt[q * REACH : (q + 1) * REACH]
             cent[pl.ds(start, REACH), :] = vc[q * REACH : (q + 1) * REACH]
 
-    repeat(rows, 4, load_row)
+    repeat(rows, 8, load_row)
 
     above = (lat + n_lat - 1) // n_lat
     below = (2 * n_lat - 2 - lat) // n_lat
@@ -304,7 +304,7 @@
         v = jnp.transpose(jnp.concatenate(pieces, axis=0))
         out_ref[pl.ds(r, members, stride=rows), :] = v[:members]
 
-    repeat(rows, 4, store_row)
+    repeat(rows, 8, store_row)
 
 
 def local(ensemble, obs_value, obs_error, obs_cell, obs_radius, obs_count, batch_order):

time: 49.4 us -> 48.7 us (0.986)
  Pallas kernels: 42.4 us -> 41.7 us
    pallas_call x1, Pallas kernels: 42.4 us -> 41.7 us  [local(): pl.pallas_call(functools.partial(kernel, (members, rows, cols, slots, bat...]
where the time goes in v4:
time: 48.7 us; the launch traced here: 48.2 us
  Pallas kernels  41.7 us (86%)
  local copies, waits for them, and re-layouts  6.49 us (13%)
    pallas_call x1, Pallas kernels, local(): pl.pallas_call(functools.partial(kernel, (members, rows, cols, slots, bat...  41.7 us
    unnamed x14, local copies, waits for them, and re-layouts  6.49 us

profile of v4, /device:TPU:17, one launch (start us, length us, event | category | flops | bytes accessed | tf_op | source)
XLA Modules:
  0.0 48.2 jit_solution(2821640379704323726)
XLA Ops:
  0.0 0.7 %copy.8.count_s = s32[4,1,1]{2,1,0:T(1,128)S(1)} copy(s32[4,1,1]{0,2,1:T(1,128)} %param.12) | data formatting | bytes 32 | tf_op args[5]
  0.7 0.0 copy-start
  0.7 1.3 %copy-done = f32[80,1,32,128]{3,2,1,0:T(8,128)S(1)} copy-done((f32[80,1,32,128]{3,2,1,0:T(8,128)S(1)}, f32[80,1,32,128]{3,2,1,0:T(8,128)}, u32[]{:S(2)}) %copy-start) | copy-done | bytes 1310744
  2.1 0.0 copy-start.1
  2.1 0.7 %copy-done.1 = s32[4,1,1,128]{3,2,1,0:T(1,128)S(1)} copy-done((s32[4,1,1,128]{3,2,1,0:T(1,128)S(1)}, s32[4,1,1,128]{3,2,1,0:T(1,128)}, u32[]{:S(2)}) %copy-start.1) | copy-done | bytes 2072
  2.7 0.0 copy-start.2
  2.7 0.7 %copy-done.2 = f32[4,1,1,128]{3,2,1,0:T(1,128)S(1)} copy-done((f32[4,1,1,128]{3,2,1,0:T(1,128)S(1)}, f32[4,1,1,128]{3,2,1,0:T(1,128)}, u32[]{:S(2)}) %copy-start.2) | copy-done | bytes 2072
  3.4 0.0 copy-start.3
  3.4 0.7 %copy-done.3 = f32[4,1,1,128]{3,2,1,0:T(1,128)S(1)} copy-done((f32[4,1,1,128]{3,2,1,0:T(1,128)S(1)}, f32[4,1,1,128]{3,2,1,0:T(1,128)}, u32[]{:S(2)}) %copy-start.3) | copy-done | bytes 2072
  4.1 0.0 copy-start.4
  4.1 0.7 %copy-done.4 = s32[4,1,1,128]{3,2,1,0:T(1,128)S(1)} copy-done((s32[4,1,1,128]{3,2,1,0:T(1,128)S(1)}, s32[4,1,1,128]{3,2,1,0:T(1,128)}, u32[]{:S(2)}) %copy-start.4) | copy-done | bytes 2072
  4.8 0.0 copy-start.5
  4.8 0.7 %copy-done.5 = s32[4]{0:T(128)S(1)} copy-done((s32[4]{0:T(128)S(1)}, s32[4]{0:T(128)}, u32[]{:S(2)}) %copy-start.5) | copy-done | bytes 40
  5.4 41.7 %shard_map.73 = f32[2560,128]{1,0:T(8,128)S(1)} custom-call(s32[4]{0:T(128)S(1)} %copy-done.5, s32[4,1,1]{2,1,0:T(1,128)S(1)} %copy.8.count_s, s32[4,1,1,128]{3,2,1,0:T(1,128)S(1)} %copy-done.1, f32[2560,128]{1,0:T(8,128)S(1)} %bitcast.5, f32[4,1,1,128]{3,2,1,0:T(1,128)S(1)} %copy-done.2, f32[4,1,1,128]{3,2,1,0:T(1,128)S(1)} %copy-done.3, ...), custom_call_target="tpu_custom_call" | custom-call | tf_op jit(solution)/shard_map/pallas_call | solution.py:322
  47.2 1.1 %copy.11 = f32[80,1,32,128]{3,2,1,0:T(8,128)} copy(f32[80,1,32,128]{3,2,1,0:T(8,128)S(1)} %bitcast.4) | data formatting | bytes 2621440
Async XLA Ops:
  0.7 1.3 %copy-start = (f32[80,1,32,128]{3,2,1,0:T(8,128)S(1)}, f32[80,1,32,128]{3,2,1,0:T(8,128)}, u32[]{:S(2)}) copy-start(f32[80,1,32,128]{3,2,1,0:T(8,128)} %param.7) | copy-start | bytes 3932164
  2.1 0.7 %copy-start.1 = (s32[4,1,1,128]{3,2,1,0:T(1,128)S(1)}, s32[4,1,1,128]{3,2,1,0:T(1,128)}, u32[]{:S(2)}) copy-start(s32[4,1,1,128]{3,2,1,0:T(1,128)} %cell_ref.1) | copy-start | bytes 6148
  2.7 0.7 %copy-start.2 = (f32[4,1,1,128]{3,2,1,0:T(1,128)S(1)}, f32[4,1,1,128]{3,2,1,0:T(1,128)}, u32[]{:S(2)}) copy-start(f32[4,1,1,128]{3,2,1,0:T(1,128)} %value_ref.1) | copy-start | bytes 6148
  3.4 0.7 %copy-start.3 = (f32[4,1,1,128]{3,2,1,0:T(1,128)S(1)}, f32[4,1,1,128]{3,2,1,0:T(1,128)}, u32[]{:S(2)}) copy-start(f32[4,1,1,128]{3,2,1,0:T(1,128)} %error_ref.1) | copy-start | bytes 6148
  4.1 0.7 %copy-start.4 = (s32[4,1,1,128]{3,2,1,0:T(1,128)S(1)}, s32[4,1,1,128]{3,2,1,0:T(1,128)}, u32[]{:S(2)}) copy-start(s32[4,1,1,128]{3,2,1,0:T(1,128)} %radius_ref.1) | copy-start | bytes 6148
  4.8 0.7 %copy-start.5 = (s32[4]{0:T(128)S(1)}, s32[4]{0:T(128)}, u32[]{:S(2)}) copy-start(s32[4]{0:T(128)} %order_s.1) | copy-start | bytes 52
